TPU v7x, 32 devices: a whole 2x2x4 slice. The times are simulated.
32 devices in a mesh: req: 8 (over z, x), head: 4 (over y, core).
Axes of the slice: x: 2, y: 2, z: 4, core: 2. Of those that a mesh axis runs over, the one named last changes fastest.
Arguments:
- hidden_state: bfloat16 [64, 2048], P('req'), may hold values from -6 to 6
- attend_gain: float32 [2048], replicated, may hold values from 0.1 to 1.9
- input_weight: bfloat16 [2048, 3, 2048], P(None, None, 'head'), may hold values from -0.125 to 0.125
- input_bias: float32 [3, 2048], P(None, 'head'), may hold values from -3 to 3
- output_weight: bfloat16 [2048, 2048], P('head'), may hold values from -0.125 to 0.125
- window_cache: bfloat16 [64, 2, 2048, 2048], P('req', None, None, 'head'), may hold values from -9 to 9
- sink_cache: bfloat16 [64, 2, 4, 2048], P('req', None, None, 'head'), may hold values from -3000 to 3000
- lengths: int32 [64], P('req'), may hold values from 16 to 32768, as said below
- expert_index: int32 [64, 4], P('req'), may hold values from 0 to 31, all different within a row; in each aligned block of 8 rows (0 to 7, 8 to 15, ...) at most 2 rows name the same one
- router_weight: float32 [64, 4], P('req'), may hold values from 0.05 to 0.5
- mixture_gain: float32 [2048], replicated, may hold values from 0.1 to 1.9
- expert_gate_up: bfloat16 [2, 45056, 2048], P(None, ('req', 'head')), may hold values from -0.125 to 0.125
- expert_down: bfloat16 [45056, 2048], P(('req', 'head')), may hold values from -0.3125 to 0.3125
- shared_gate_up: bfloat16 [2, 2048, 5632], P(None, 'req', 'head'), may hold values from -0.125 to 0.125
- shared_down: bfloat16 [5632, 2048], P('head', 'req'), may hold values from -0.078125 to 0.078125
- shared_gate: float32 [2048], replicated, may hold values from -0.125 to 0.125
Outputs:
- layer_out: bfloat16 [64, 2048], P('req', 'head')
- new_kv: bfloat16 [64, 2, 2048], P('req', None, 'head')
Inputs may be any that keep to these rules, and one draw needn't show every extreme that they name: Request r has lengths[r] cached tokens and its new token takes position lengths[r]; some request has exactly 32768 cached tokens and some has 16. `expert_index`: each row names 4 different experts; within the rows of one index of req (aligned blocks of 8 rows) no expert is named more than 2 times, a bound that some block reaches.
All inputs are finite; a program needn't handle non-finite values.
Results may differ from a plain program's by a relative error of at most 0.014.
The roundings to bfloat16 on the way count: a program that leaves them out, or rounds other values in their place, can miss the bound.
Values may be sent and summed in bfloat16 or wider, within the bound.
No kernel may reach another device: no remote copies, remote signals or barrier semaphores. Data moves between devices by JAX's collectives and lax.ppermute only.
A program may use at most 256 MiB of HBM per device.

v0:
```python
import math

import jax
import jax.numpy as jnp
from jax import lax
from jax.sharding import PartitionSpec as P

HD = 128
EXPERTS = 32
FE = 1408
SINKS = 4
CAP = 2


EPSILON = 1e-06
ROPE_BASE = 1000000.0


def rms_scale(values, gains):
    mean_square = jnp.mean(values * values, axis=-1, keepdims=True)
    return values * lax.rsqrt(mean_square + EPSILON) * gains


def rotate(vectors, positions):
    half_depth = vectors.shape[-1] // 2
    steps_half = jnp.arange(half_depth).astype(jnp.float32)
    frequencies = jnp.float32(ROPE_BASE) ** (-(2.0 / vectors.shape[-1]) * steps_half)
    angles = positions.astype(jnp.float32)[:, None] * frequencies[None, :]
    cosine = jnp.cos(angles)[:, None, :]
    sine_terms = jnp.sin(angles)[:, None, :]
    lower_half = vectors[..., :half_depth]
    upper_half = vectors[..., half_depth:]
    return jnp.concatenate(
        [
            lower_half * cosine - upper_half * sine_terms,
            upper_half * cosine + lower_half * sine_terms,
        ],
        axis=-1,
    )


def block_scores(queries, fresh_key, window_cache, fresh_slot, live_count, block_size):
    row_count, head_count, head_depth = queries.shape
    key_rows = window_cache[:, 0].reshape(row_count, block_size, head_count, head_depth)
    scores = jnp.einsum("rhd,rshd->rhs", queries, key_rows, preferred_element_type=jnp.float32)
    fresh_scores = jnp.einsum("rhd,rhd->rh", queries, fresh_key, preferred_element_type=jnp.float32)
    positions = jnp.arange(block_size)
    is_fresh = positions[None, :] == fresh_slot[:, None]
    scores = jnp.where(is_fresh[:, None, :], fresh_scores[:, :, None], scores) / math.sqrt(
        head_depth
    )
    keeping = positions[None, :] < live_count[:, None]
    return jnp.where(keeping[:, None, :], scores, -jnp.inf)


def block_values(window_cache, block_size, head_count, head_depth):
    row_count = window_cache.shape[0]
    return window_cache[:, 1].reshape(row_count, block_size, head_count, head_depth)


def window_values(weights, is_fresh, value_rows, fresh_value):
    kept_weights = jnp.where(is_fresh[:, None, :], jnp.zeros_like(weights), weights)
    fresh_weight = jnp.sum(
        jnp.where(is_fresh[:, None, :], weights, jnp.zeros_like(weights)), axis=-1
    )
    window_part = jnp.einsum(
        "rhs,rshd->rhd", kept_weights, value_rows, preferred_element_type=jnp.float32
    )
    return window_part + fresh_weight.astype(jnp.float32)[..., None] * fresh_value.astype(
        jnp.float32
    )


def expert_slice(arrived, expert_gate_up, expert_down):
    gate_terms = jnp.einsum(
        "nkd,fd->nkf", arrived, expert_gate_up[0], preferred_element_type=jnp.float32
    )
    up_terms = jnp.einsum(
        "nkd,fd->nkf", arrived, expert_gate_up[1], preferred_element_type=jnp.float32
    )
    hidden_units = (jax.nn.silu(gate_terms) * up_terms).astype(jnp.bfloat16)
    return jnp.einsum("nkf,fd->nkd", hidden_units, expert_down, preferred_element_type=jnp.float32)


def local(
    hidden_state,
    attend_gain,
    input_weight,
    input_bias,
    output_weight,
    window_cache,
    sink_cache,
    lengths,
    expert_index,
    router_weight,
    mixture_gain,
    expert_gate_up,
    expert_down,
    shared_gate_up,
    shared_down,
    shared_gate,
):
    row_count, model_width = hidden_state.shape
    local_width = input_weight.shape[2]
    head_depth = HD
    head_count = local_width // head_depth
    window_length = window_cache.shape[2]
    normed = rms_scale(hidden_state.astype(jnp.float32), attend_gain).astype(jnp.bfloat16)
    projected = jnp.dot(
        normed,
        input_weight.reshape(model_width, 3 * local_width),
        preferred_element_type=jnp.float32,
    ) + input_bias.reshape(3 * local_width)
    projected = projected.reshape(row_count, 3, head_count, head_depth)
    queries = rotate(projected[:, 0], lengths).astype(jnp.bfloat16)
    fresh_key = rotate(projected[:, 1], lengths).astype(jnp.bfloat16)
    fresh_value = projected[:, 2].astype(jnp.bfloat16)
    new_kv = jnp.stack(
        [fresh_key.reshape(row_count, local_width), fresh_value.reshape(row_count, local_width)],
        axis=1,
    )
    fresh_slot = (lengths - SINKS) % window_length
    live_count = jnp.minimum(lengths - SINKS + 1, window_length)
    sink_keys = sink_cache[:, 0].reshape(row_count, SINKS, head_count, head_depth)
    sink_values = sink_cache[:, 1].reshape(row_count, SINKS, head_count, head_depth)
    sink_scores = jnp.einsum(
        "rhd,rshd->rhs", queries, sink_keys, preferred_element_type=jnp.float32
    ) / math.sqrt(head_depth)
    scores = block_scores(queries, fresh_key, window_cache, fresh_slot, live_count, window_length)
    is_fresh = jnp.arange(window_length)[None, :] == fresh_slot[:, None]
    value_rows = block_values(window_cache, window_length, head_count, head_depth)
    score_peak = jnp.maximum(jnp.max(sink_scores, axis=-1), jnp.max(scores, axis=-1))
    window_exp = jnp.exp(scores - score_peak[..., None])
    score_total = jnp.sum(jnp.exp(sink_scores - score_peak[..., None]), axis=-1) + jnp.sum(
        window_exp, axis=-1
    )
    weights = (window_exp / score_total[..., None]).astype(jnp.bfloat16)
    accum = window_values(weights, is_fresh, value_rows, fresh_value)
    sink_weights = (jnp.exp(sink_scores - score_peak[..., None]) / score_total[..., None]).astype(
        jnp.bfloat16
    )
    accum = accum + jnp.einsum(
        "rhs,rshd->rhd", sink_weights, sink_values, preferred_element_type=jnp.float32
    )
    attended = accum.astype(jnp.bfloat16).reshape(row_count, local_width)
    attend_part = jnp.dot(attended, output_weight, preferred_element_type=jnp.float32)
    resid = hidden_state.astype(jnp.float32) + lax.psum(attend_part, "head")
    tokens = rms_scale(resid, mixture_gain).astype(jnp.bfloat16)
    all_tokens = lax.all_gather(tokens, "req", axis=0, tiled=True)
    group_index = lax.axis_index("req")
    group_count = lax.axis_size("req")
    row_width = shared_gate_up.shape[1]
    my_columns = lax.dynamic_slice_in_dim(all_tokens, group_index * row_width, row_width, 1)
    shared_terms = jnp.einsum(
        "td,cdf->ctf", my_columns, shared_gate_up, preferred_element_type=jnp.float32
    )
    shared_terms = lax.psum(shared_terms, "req")
    shared_hidden = (jax.nn.silu(shared_terms[0]) * shared_terms[1]).astype(jnp.bfloat16)
    gate_value = jax.nn.sigmoid(
        jnp.dot(all_tokens.astype(jnp.float32), shared_gate, precision=lax.Precision.HIGHEST)
    )
    shared_out = gate_value[:, None] * jnp.dot(
        shared_hidden, shared_down, preferred_element_type=jnp.float32
    )
    expert_hot = (expert_index[:, :, None] == jnp.arange(EXPERTS)[None, None, :]).astype(
        jnp.float32
    )
    combine = jnp.sum(expert_hot * router_weight[:, :, None], axis=1)
    local_experts = EXPERTS // group_count
    quarters = FE // expert_down.shape[0]
    local_pick = lax.axis_index("head") // quarters
    expert_hit = jnp.sum(expert_hot, axis=1)
    slot_rank = jnp.cumsum(expert_hit, axis=0) - expert_hit
    chosen = expert_hit[:, :, None] * (
        slot_rank[:, :, None] == jnp.arange(CAP)[None, None, :]
    ).astype(jnp.float32)
    mine_hot = (jnp.arange(local_experts) == local_pick).astype(jnp.float32)
    chosen_mine = jnp.einsum(
        "rglc,l->rgc",
        chosen.reshape(row_count, group_count, local_experts, CAP),
        mine_hot,
        precision=lax.Precision.HIGHEST,
    )
    combine_mine = jnp.einsum(
        "rgl,l->rg",
        combine.reshape(row_count, group_count, local_experts),
        mine_hot,
        precision=lax.Precision.HIGHEST,
    )
    placing = chosen_mine.reshape(row_count, group_count * CAP)
    outgoing = jnp.dot(
        placing.T.astype(jnp.bfloat16), tokens, preferred_element_type=jnp.float32
    ).astype(jnp.bfloat16)
    outgoing = outgoing.reshape(group_count, CAP, model_width)
    produced = expert_slice(
        lax.all_to_all(outgoing, "req", split_axis=0, concat_axis=0, tiled=True),
        expert_gate_up,
        expert_down,
    )
    returned = lax.all_to_all(produced, "req", split_axis=0, concat_axis=0, tiled=True)
    weighting = (chosen_mine * combine_mine[:, :, None]).reshape(row_count, group_count * CAP)
    routed = jnp.dot(
        weighting,
        returned.reshape(group_count * CAP, model_width),
        precision=lax.Precision.HIGHEST,
        preferred_element_type=jnp.float32,
    )
    routed = routed + lax.all_to_all(shared_out, "req", split_axis=0, concat_axis=1, tiled=True)
    final = lax.psum_scatter(routed, "head", scatter_dimension=1, tiled=True)
    slice_width = final.shape[1]
    own_resid = lax.dynamic_slice_in_dim(
        resid, lax.axis_index("head") * slice_width, slice_width, 1
    )
    return ((own_resid + final).astype(jnp.bfloat16), new_kv)


def solution(mesh):
    return jax.shard_map(
        local,
        mesh=mesh,
        in_specs=(
            P("req", None),
            P(),
            P(None, None, "head"),
            P(None, "head"),
            P("head", None),
            P("req", None, None, "head"),
            P("req", None, None, "head"),
            P("req"),
            P("req", None),
            P("req", None),
            P(),
            P(None, ("req", "head"), None),
            P(("req", "head"), None),
            P(None, "req", "head"),
            P("head", "req"),
            P(),
        ),
        out_specs=(P("req", "head"), P("req", None, "head")),
        check_vma=False,
    )
```

profile of v0, /device:TPU:0, one launch (start us, length us, event | category | flops | bytes accessed | tf_op | source)
XLA Modules:
  0.0 306.4 jit_solution(18246826656507924227)
XLA Ops:
  7.2 0.0 all-reduce.3.cloned.1.call-start
  7.3 0.8 and_select_fusion
  8.1 8.8 %copy.43 = bf16[2048,3,512]{0,2,1:T(8,128)(2,1)} copy(bf16[2048,3,512]{2,0,1:T(8,128)(2,1)} %param.18) | data formatting | bytes 12582912 | tf_op args[2]
  16.9 0.1 fusion.39
  17.1 4.5 %convolution_add_fusion = f32[8,1536]{1,0:T(8,128)S(1)} fusion(bf16[2048,1536]{0,1:T(8,128)(2,1)} %bitcast.145, bf16[8,2048]{1,0:T(8,128)(2,1)S(1)} %copy-done.4, f32[2048]{0:T(1024)S(1)} %copy-done.7, f32[8]{0:T(128)S(1)} %add_rsqrt_fusion.1, f32[1536]{0:T(1024)S(1)} %add.96), kind=kOutput, calls=%fused_computation.14 | convolution fusion | flops 50409472 | bytes 6387744 | tf_op jit(solution)/shard_map/dot_general | solution.py:109
  21.6 0.6 copy-done.5
  22.2 0.1 multiply_cosine_fusion
  22.3 0.1 subtract_convert_fusion
  22.4 0.1 multiply_subtract_fusion
  22.5 22.5 %fusion.80 = (bf16[8,1,2048,512]{3,2,1,0:T(8,128)(2,1)}, bf16[8,1,2048,512]{3,2,1,0:T(8,128)(2,1)}) fusion(bf16[8,2,2048,512]{3,2,1,0:T(8,128)(2,1)} %param.21), kind=kLoop, calls=%fused_computation.124 | loop fusion | bytes 67108864 | tf_op jit(solution)/shard_map/slice | solution.py:58
  45.0 21.6 %copy.77 = bf16[8,1,2048,512]{2,3,0,1:T(8,128)(2,1)} copy(bf16[8,1,2048,512]{3,2,1,0:T(8,128)(2,1)} %get-tuple-element.17) | data formatting | bytes 33554432 | tf_op jit(solution)/shard_map/reshape;squeeze | solution.py:44
  66.6 0.1 fusion.72
  66.7 8.0 %fusion.58 = f32[8,4,1,2048]{3,2,1,0:T(1,128)S(1)} fusion(bf16[8,2048,4,128]{1,3,2,0:T(8,128)(2,1)} %bitcast.144, bf16[8,4,128,1]{2,0,1,3:T(8,128)(2,1)S(1)} %fusion.72), kind=kOutput, calls=%fused_computation.87 | convolution fusion | flops 16777216 | bytes 17047552 | tf_op jit(solution)/shard_map/rhd,rshd->rhs/dot_general | solution.py:45
  74.8 0.2 fusion.51
  74.9 0.1 copy.62
  75.0 0.7 fusion.56
  75.7 0.1 iota_compare_fusion
  75.8 0.3 fusion.32
  76.1 0.3 fusion.29
  76.5 0.3 select_reduce_fusion
  76.8 0.7 select_bitcast_fusion
  77.5 23.7 %reshape_squeeze.14 = bf16[8,2048,4,128]{3,2,1,0:T(4,128)(2,1)} reshape(bf16[8,1,2048,512]{3,2,1,0:T(8,128)(2,1)} %get-tuple-element.16) | data formatting | bytes 33554432 | tf_op jit(solution)/shard_map/reshape;squeeze | solution.py:58
  101.1 0.1 copy.66
  101.3 0.1 fusion.52
  101.4 8.3 %fusion = f32[8,4,1,128]{3,2,1,0:T(1,128)S(1)} fusion(bf16[8,2048,4,128]{3,2,1,0:T(4,128)(2,1)} %reshape_squeeze.14, bf16[8,4,2048,1]{2,0,1,3:T(8,128)(2,1)} %select_bitcast_fusion), kind=kOutput, calls=%fused_computation | convolution fusion | flops 16777216 | bytes 16924672 | tf_op jit(solution)/shard_map/rhs,rshd->rhd/dot_general | solution.py:66
  109.8 1.8 fusion.61
  111.6 0.5 iota_convert_fusion
  112.1 0.7 select_reduce_fusion.1
  112.8 0.8 copy.44
  113.5 0.7 copy.46
  114.3 3.2 %reduce_window_sum.14 = f32[8,8,4]{0,2,1:T(4,128)} reduce-window(f32[8,8,4]{0,2,1:T(4,128)S(1)} %bitcast.147, f32[]{:T(128)} %constant.67.clone.1), window={size=8x1x1 pad=7_0x0_0x0_0}, to_apply=%region_8.9 | reduce-window | flops 1792 | bytes 2052 | tf_op jit(solution)/shard_map/jit(cumsum)/reduce_window_sum | solution.py:173
  117.4 1.3 sub.46
  118.8 1.4 copy.45
  120.2 1.6 multiply_reduce_fusion
  121.8 1.5 copy.74
  123.3 0.7 copy.47
  124.0 0.1 fusion.70
  124.2 0.8 broadcast_multiply_fusion
  124.9 20.5 %all-reduce.3.cloned.1.call-done = f32[8,2048]{1,0:T(8,128)} async-done(((f32[8,2048]{1,0:T(8,128)}), f32[8,2048]{1,0:T(8,128)}) %all-reduce.3.cloned.1.call-update) | async-done | bytes 65552 | tf_op jit(solution)/shard_map/psum | solution.py:147
  145.5 1.0 multiply_reduce_fusion.1
  146.4 0.6 copy-done.3
  147.0 0.8 multiply_convert_fusion
  147.8 32.8 %all_gather.3 = bf16[64,2048]{1,0:T(8,128)(2,1)} all-gather(bf16[8,2048]{1,0:T(8,128)(2,1)S(1)} %multiply_convert_fusion), channel_id=1, replica_groups=mesh['req'=8,'head'=4] {'req'}, dimensions={0}, use_global_device_ids=true | all-gather | bytes 294912 | tf_op jit(solution)/shard_map/all_gather | solution.py:149
  180.6 0.8 convolution_convert_fusion
  181.4 1.5 reshape.198
  182.9 5.4 %all-to-all-start = ((bf16[8,2,2048]{2,1,0:T(2,128)(2,1)}), bf16[8,2,2048]{2,1,0:T(2,128)(2,1)}, u32[]{:S(2)}, u32[]{:S(2)}) async-start(bf16[8,2,2048]{2,1,0:T(2,128)(2,1)} %reshape.198), calls=%async_computation | async-start | bytes 131072 | tf_op jit(solution)/shard_map/all_to_all | solution.py:196
  188.3 0.2 all-reduce.5.cloned.1.call-start
  188.6 2.0 convolution_bitcast_fusion
  190.6 4.7 %all-to-all-done = bf16[8,2,2048]{2,1,0:T(2,128)(2,1)} async-done(((bf16[8,2,2048]{2,1,0:T(2,128)(2,1)}), bf16[8,2,2048]{2,1,0:T(2,128)(2,1)}, u32[]{:S(2)}, u32[]{:S(2)}) %all-to-all-start) | async-done | bytes 65568 | tf_op jit(solution)/shard_map/all_to_all | solution.py:196
  195.3 4.3 %fusion.6 = f32[8,2,1408]{2,0,1:T(8,128)S(1)} fusion(bf16[2,1408,2048]{2,1,0:T(8,128)(2,1)} %param.27, bf16[8,2,2048]{2,1,0:T(2,128)(2,1)} %all-to-all-done), kind=kOutput, calls=%fused_computation.6 | convolution fusion | flops 92274688 | bytes 5922816 | tf_op jit(solution)/shard_map/nkd,fd->nkf/dot_general | solution.py:75
  199.6 7.1 %fusion.2 = f32[8,2,2048]{2,0,1:T(8,128)S(1)} fusion(bf16[1408,2048]{1,0:T(8,128)(2,1)} %param.28, bf16[2,1408,2048]{2,1,0:T(8,128)(2,1)} %param.27, f32[8,2,1408]{2,0,1:T(8,128)S(1)} %fusion.6, bf16[8,2,2048]{2,1,0:T(2,128)(2,1)} %all-to-all-done), kind=kOutput, calls=%fused_computation.2 | convolution fusion | flops 184684544 | bytes 11821056 | tf_op jit(solution)/shard_map/nkf,fd->nkd/dot_general | solution.py:82
  206.6 0.8 copy.50
  207.4 3.4 %all-to-all-start.1 = ((f32[8,2,2048]{2,1,0:T(2,128)}), f32[8,2,2048]{2,1,0:T(2,128)S(1)}, u32[]{:S(2)}, u32[]{:S(2)}) async-start(f32[8,2,2048]{2,1,0:T(2,128)} %copy.50), calls=%async_computation.1 | async-start | bytes 262144 | tf_op jit(solution)/shard_map/all_to_all | solution.py:200
  210.8 0.0 reduce-scatter.2.cloned.1.call-start
  210.9 0.3 fusion.21
  211.2 57.6 %all-reduce.5.cloned.1.call-done = f32[2,64,1408]{2,1,0:T(8,128)} async-done(((f32[2,64,1408]{2,1,0:T(8,128)}), f32[2,64,1408]{2,1,0:T(8,128)}) %all-reduce.5.cloned.1.call-update) | async-done | bytes 720912 | tf_op jit(solution)/shard_map/psum | solution.py:157
  268.7 1.4 fusion.17
  270.1 10.4 %all_to_all.29 = f32[8,8,256]{2,1,0:T(8,128)S(1)} all-to-all(f32[8,8,256]{2,1,0:T(8,128)S(1)} %fusion.17), channel_id=1, replica_groups=mesh['req'=8,'head'=4] {'req'}, dimensions={0} | all-to-all | bytes 131072 | tf_op jit(solution)/shard_map/all_to_all | solution.py:208
  280.5 0.9 fusion.16
  281.4 0.0 reduce-scatter.2.cloned.1.call-update
  281.4 0.7 fusion.69
  282.2 0.6 copy.53
  282.8 15.7 %reduce-scatter.2.cloned.1.call-done = f32[8,512]{1,0:T(8,128)} async-done(((f32[8,2048]{1,0:T(8,128)}), f32[8,512]{1,0:T(8,128)}) %reduce-scatter.2.cloned.1.call-update) | async-done | bytes 16400 | tf_op jit(solution)/shard_map/reduce_scatter | solution.py:209
  298.5 1.3 add_convert_fusion
  (42 shorter events, 0.2 us)
Async XLA Ops:
  7.2 102.6 %copy-start = (bf16[512,2048]{1,0:T(8,128)(2,1)S(1)}, bf16[512,2048]{1,0:T(8,128)(2,1)}, u32[]{:S(2)}) copy-start(bf16[512,2048]{1,0:T(8,128)(2,1)} %param.20) | copy-start | bytes 6291460
  7.2 9.7 %copy-start.8 = (f32[3,512]{1,0:T(4,128)S(1)}, f32[3,512]{1,0:T(4,128)}, u32[]{:S(2)}) copy-start(f32[3,512]{1,0:T(4,128)} %param.19) | copy-start | bytes 18436
  7.2 9.7 %copy-start.4 = (bf16[8,2048]{1,0:T(8,128)(2,1)S(1)}, bf16[8,2048]{1,0:T(8,128)(2,1)}, u32[]{:S(2)}) copy-start(bf16[8,2048]{1,0:T(8,128)(2,1)} %param.16) | copy-start | bytes 98308
  7.2 9.9 %copy-start.7 = (f32[2048]{0:T(1024)S(1)}, f32[2048]{0:T(1024)}, u32[]{:S(2)}) copy-start(f32[2048]{0:T(1024)} %param.17) | copy-start | bytes 24580
  7.2 138.2 %all-reduce.3.cloned.1.call-start = ((), (), s32[]{:S(2)}) async-start(), calls=%async_computation.4 | async-start | bytes 131072 | tf_op jit(solution)/shard_map/psum | solution.py:147
  21.6 0.6 copy-start.5
  66.6 8.1 %copy-start.12 = (bf16[8,2,4,512]{3,2,1,0:T(4,128)(2,1)S(1)}, bf16[8,2,4,512]{3,2,1,0:T(4,128)(2,1)}, u32[]{:S(2)}) copy-start(bf16[8,2,4,512]{3,2,1,0:T(4,128)(2,1)} %param.22) | copy-start | bytes 196612
  101.4 10.7 %copy-start.9 = (f32[8,4]{0,1:T(4,128)S(1)}, f32[8,4]{0,1:T(4,128)}, u32[]{:S(2)}) copy-start(f32[8,4]{0,1:T(4,128)} %param.25) | copy-start | bytes 388
  101.4 10.7 %copy-start.10 = (s32[8,4]{0,1:T(4,128)S(1)}, s32[8,4]{0,1:T(4,128)}, u32[]{:S(2)}) copy-start(s32[8,4]{0,1:T(4,128)} %param.24) | copy-start | bytes 388
  101.4 87.1 %copy-start.1 = (bf16[2,256,1408]{2,1,0:T(8,128)(2,1)S(1)}, bf16[2,256,1408]{2,1,0:T(8,128)(2,1)}, u32[]{:S(2)}) copy-start(bf16[2,256,1408]{2,1,0:T(8,128)(2,1)} %param.29) | copy-start | bytes 4325380
  146.4 0.6 copy-start.3
  182.9 12.4 %all-to-all-start = ((bf16[8,2,2048]{2,1,0:T(2,128)(2,1)}), bf16[8,2,2048]{2,1,0:T(2,128)(2,1)}, u32[]{:S(2)}, u32[]{:S(2)}) async-start(bf16[8,2,2048]{2,1,0:T(2,128)(2,1)} %reshape.198), calls=%async_computation | async-start | bytes 131072 | tf_op jit(solution)/shard_map/all_to_all | solution.py:196
  188.3 80.4 %all-reduce.5.cloned.1.call-start = ((), (), s32[]{:S(2)}) async-start(), calls=%async_computation.5 | async-start | bytes 1441792 | tf_op jit(solution)/shard_map/psum | solution.py:157
  190.6 20.3 %copy-start.2 = (bf16[64,2048]{1,0:T(8,128)(2,1)S(1)}, bf16[64,2048]{1,0:T(8,128)(2,1)}, u32[]{:S(2)}) copy-start(bf16[64,2048]{1,0:T(8,128)(2,1)} %all_gather.3) | copy-start | bytes 786436
  190.6 20.3 %copy-start.13 = (f32[2048]{0:T(1024)S(1)}, f32[2048]{0:T(1024)}, u32[]{:S(2)}) copy-start(f32[2048]{0:T(1024)} %param.31) | copy-start | bytes 24580
  190.6 78.1 %copy-start.11 = (bf16[1408,256]{1,0:T(8,128)(2,1)S(1)}, bf16[1408,256]{1,0:T(8,128)(2,1)}, u32[]{:S(2)}) copy-start(bf16[1408,256]{1,0:T(8,128)(2,1)} %param.30) | copy-start | bytes 2162692
  190.6 91.5 %copy-start.6 = (bf16[8,4,128]{2,0,1:T(8,128)(2,1)S(1)}, bf16[8,4,128]{2,0,1:T(8,128)(2,1)}, u32[]{:S(2)}) copy-start(bf16[8,4,128]{2,0,1:T(8,128)(2,1)} %get-tuple-element.15) | copy-start | bytes 24580
  207.4 62.7 %all-to-all-start.1 = ((f32[8,2,2048]{2,1,0:T(2,128)}), f32[8,2,2048]{2,1,0:T(2,128)S(1)}, u32[]{:S(2)}, u32[]{:S(2)}) async-start(f32[8,2,2048]{2,1,0:T(2,128)} %copy.50), calls=%async_computation.1 | async-start | bytes 262144 | tf_op jit(solution)/shard_map/all_to_all | solution.py:200
  210.8 87.7 %reduce-scatter.2.cloned.1.call-start = ((), (), s32[]{:S(2)}) async-start(), calls=%async_computation.6 | async-start | bytes 81920 | tf_op jit(solution)/shard_map/reduce_scatter | solution.py:209
Sparse Core Ops, SparseCore 0:
  111.7 33.7 all-reduce.2
  193.1 75.6 all-reduce.4
  281.6 16.9 reduce-scatter.1
where the time goes:
time: 309 us; the launch traced here: 306 us
  waiting for transfers between devices  98.6 us (32%)
  local copies, waits for them, and re-layouts  86.9 us (28%)
  blocking collectives  43.2 us (14%)
  matrix products  39.7 us (13%)
  other arithmetic  14.9 us (5%)
  between operations  14 us (5%)
  starting transfers between devices  9.11 us (3%)
    psum x1, waiting for transfers between devices, local(): shared_terms = lax.psum(shared_terms, 'req')  57.6 us
    all_gather x1, blocking collectives, local(): all_tokens = lax.all_gather(tokens, 'req', axis=0, tiled=True)  32.8 us
    another operation x1, local copies, waits for them, and re-layouts, block_values(): window_cache[:, 1].reshape(row_count, block_size, head_count, head_depth)  23.7 us
    slice x1, local copies, waits for them, and re-layouts, block_values(): window_cache[:, 1].reshape(row_count, block_size, head_count, head_depth)  22.5 us
    another operation x1, local copies, waits for them, and re-layouts, block_scores(): window_cache[:, 0].reshape(row_count, block_size, head_count, head_depth)  21.6 us
    psum x1, waiting for transfers between devices, local(): resid = hidden_state.astype(jnp.float32) + lax.psum(attend_part, 'head')  20.5 us
    reduce_scatter x1, waiting for transfers between devices, local(): final = lax.psum_scatter(routed, 'head', scatter_dimension=1, tiled=True)  15.7 us
    unnamed x30, local copies, waits for them, and re-layouts  10.8 us
  transfers between devices with their start and end apart: 5, of which 4 were waited for; matrix products, arithmetic and copies ran while one was open for 10% of the time, Pallas kernels for 0%

commit v1 on v0

v1 whole, which is shorter than its diff:
```python
import functools
import math

import jax
import jax.numpy as jnp
from jax import lax
from jax.experimental import pallas as pl
from jax.experimental.pallas import tpu as pltpu
from jax.sharding import PartitionSpec as P

HD = 128
EXPERTS = 32
FE = 1408
SINKS = 4
CAP = 2
ROWS = 8

EPSILON = 1e-06
ROPE_BASE = 1000000.0
MB = 1 << 20
BF = jnp.bfloat16
F32 = jnp.float32

NT = (((1,), (1,)), ((), ()))


def iota(shape, dim):
    return lax.broadcasted_iota(jnp.int32, shape, dim)


def one(cond):
    return jnp.where(cond, 1.0, 0.0).astype(F32)


def dot(a, b):
    return jnp.dot(a, b, preferred_element_type=F32)


def split3(x):
    hi = x.astype(BF).astype(F32)
    mid = (x - hi).astype(BF).astype(F32)
    lo = (x - hi - mid).astype(BF).astype(F32)
    return jnp.concatenate([hi, mid, lo], axis=0)


def params(limit, **kw):
    return pltpu.CompilerParams(vmem_limit_bytes=limit, **kw)


VM = pl.BlockSpec(memory_space=pltpu.VMEM)
SM = pl.BlockSpec(memory_space=pltpu.SMEM)
HB = pl.BlockSpec(memory_space=pl.ANY)


def attend_kernel(
    groups,
    heads_axis,
    lens,
    hidden,
    gain,
    bias,
    cos,
    sin,
    sink_k,
    sink_v,
    idx,
    rw,
    w_hbm,
    win_hbm,
    ow_hbm,
    part,
    key_out,
    value_out,
    big_out,
    fin_out,
    w_buf,
    kv,
    ow_buf,
    qbd,
    sc,
    wts,
    acc,
    w_sem,
    kv_sem,
    ow_sem,
):
    rows, width = hidden.shape
    local = bias.shape[1]
    length = kv.shape[2]
    chunks = kv_sem.shape[2]
    ch = length // chunks
    halves = w_sem.shape[1]
    wc = width // halves

    def w_copy(c, i):
        return pltpu.make_async_copy(
            w_hbm.at[c, pl.ds(i * wc, wc)], w_buf.at[c, pl.ds(i * wc, wc)], w_sem.at[c, i]
        )

    def kv_copy(r, t, c):
        return pltpu.make_async_copy(
            win_hbm.at[r, t, pl.ds(c * ch, ch)], kv.at[r, t, pl.ds(c * ch, ch)], kv_sem.at[r, t, c]
        )

    def live_of(r):
        return jnp.minimum(lens[r] - SINKS + 1, length)

    def fetch(t):
        def step(r, carry):
            live = live_of(r)
            for c in range(chunks):

                @pl.when(c * ch < live)
                def _():
                    kv_copy(r, t, c).start()

            return carry

        lax.fori_loop(0, rows, step, 0)

    for c in range(3):
        for i in range(halves):
            w_copy(c, i).start()
    fetch(0)
    fetch(1)
    ow_copy = pltpu.make_async_copy(ow_hbm, ow_buf, ow_sem)
    ow_copy.start()

    my_head = lax.axis_index("head")
    local_experts = EXPERTS // groups
    hit = jnp.zeros((rows, EXPERTS), F32)
    comb = jnp.zeros((rows, EXPERTS), F32)
    lane_e = iota((rows, EXPERTS), 1)
    for k in range(idx.shape[1]):
        eq = one(idx[:, k : k + 1] == lane_e)
        hit = hit + eq
        comb = comb + eq * rw[:, k : k + 1]
    below = one(iota((rows, rows), 1) < iota((rows, rows), 0))
    rank = dot(below.astype(BF), hit.astype(BF))
    sel = [hit * one(rank == c) for c in range(CAP)]
    pick = my_head // (heads_axis // local_experts)
    blocks = groups
    span = rows + CAP * blocks
    total = groups * span
    row_g = iota((total, EXPERTS), 0) // span
    row_t = iota((total, EXPERTS), 0) % span
    mine = iota((total, EXPERTS), 1) == row_g * local_experts + pick
    z = jnp.zeros((total, rows), F32)
    for c in range(CAP):
        pickc = mine & (row_t >= rows) & ((row_t - rows) % CAP == c)
        z = z + lax.dot_general(
            one(pickc).astype(BF), sel[c].astype(BF), NT, preferred_element_type=F32
        )
    nb = blocks * rows
    rep = one(iota((rows, nb), 0) == iota((rows, nb), 1) % rows)
    zz = dot(z.astype(BF), rep.astype(BF))
    g2 = iota((total, nb), 0) // span
    t2 = iota((total, nb), 0) % span
    j2 = iota((total, nb), 1) // rows
    r2 = iota((total, nb), 1) % rows
    direct = one((j2 == g2) & (r2 == t2))
    placed = zz * one(j2 == (t2 - rows) // CAP)
    big_out[...] = jnp.where(t2 < rows, direct, placed).astype(BF)

    fin = fin_out.shape[1]
    fspan = fin // (groups * heads_axis)
    ratio = width // heads_axis // (width // groups)
    lane = iota((EXPERTS, fin), 1)
    dev, u = lane // fspan, lane % fspan - rows
    owner = (dev // heads_axis) * local_experts + (dev % heads_axis) // (heads_axis // local_experts)
    spread = jnp.zeros((3 * rows, fin), F32)
    for c in range(CAP):
        hot = (owner == iota((EXPERTS, fin), 0)) & (u >= c * ratio) & (u < (c + 1) * ratio)
        spread = spread + dot(split3(comb * sel[c]).astype(BF), one(hot).astype(BF))
    fin_out[...] = spread.astype(BF)

    x = hidden[...].astype(F32)
    ms = jnp.mean(x * x, axis=-1, keepdims=True)
    normed = (x * lax.rsqrt(ms + EPSILON) * gain[...]).astype(BF)
    proj = []
    for c in range(3):
        total_c = bias[c : c + 1, :]
        for i in range(halves):
            w_copy(c, i).wait()
            total_c = total_c + dot(
                normed[:, i * wc : (i + 1) * wc], w_buf[c, i * wc : (i + 1) * wc, :]
            )
        proj.append(total_c)

    def rotate(v):
        outs = []
        for h in range(local // HD):
            part_h = v[:, h * HD : (h + 1) * HD]
            outs.append(part_h * cos[...] + pltpu.roll(part_h, HD // 2, 1) * sin[...])
        return jnp.concatenate(outs, axis=1)

    q = rotate(proj[0]).astype(BF).astype(F32)
    kf = rotate(proj[1]).astype(BF)
    vf = proj[2].astype(BF)
    key_out[...] = kf
    value_out[...] = vf
    head_mask = iota((ROWS, local), 1) // HD == iota((ROWS, local), 0)
    q3 = jnp.where(head_mask[None], q[:, None, :], 0.0)
    qbd[...] = q3.astype(BF)
    fresh_scores = jnp.sum(q3 * kf.astype(F32)[:, None, :], axis=-1, keepdims=True)

    q_all = q3.reshape(rows * ROWS, local).astype(BF)
    sink_s = lax.dot_general(q_all, sink_k[...], NT, preferred_element_type=F32) / math.sqrt(HD)
    own = iota(sink_s.shape, 1) // SINKS == iota(sink_s.shape, 0) // ROWS
    sink_s = jnp.where(own, sink_s, -jnp.inf)

    def score_step(r, carry):
        used = (live_of(r) + ch - 1) // ch
        for n in range(1, chunks + 1):

            @pl.when(used == n)
            def _():
                for c in range(n):
                    kv_copy(r, 0, c).wait()
                sc[r, :, : n * ch] = lax.dot_general(
                    qbd[r], kv[r, 0, : n * ch, :], NT, preferred_element_type=F32
                )

        return carry

    lax.fori_loop(0, rows, score_step, 0)

    pos = iota((ROWS, length), 1)
    fresh_w, sink_w = [], []
    for r in range(rows):
        slot = lax.rem(lens[r] - SINKS, length)
        is_fresh = pos == slot
        s = jnp.where(is_fresh, fresh_scores[r], sc[r]) / math.sqrt(HD)
        s = jnp.where(pos < live_of(r), s, -jnp.inf)
        ss = sink_s[r * ROWS : (r + 1) * ROWS, :]
        top = jnp.maximum(
            jnp.max(s, axis=-1, keepdims=True), jnp.max(ss, axis=-1, keepdims=True)
        )
        e = jnp.exp(s - top)
        es = jnp.exp(ss - top)
        tot = jnp.sum(e, axis=-1, keepdims=True) + jnp.sum(es, axis=-1, keepdims=True)
        w = (e / tot).astype(BF).astype(F32)
        fresh_w.append(jnp.sum(jnp.where(is_fresh, w, 0.0), axis=-1, keepdims=True))
        sink_w.append(es / tot)
        wts[r] = jnp.where(is_fresh, 0.0, w).astype(BF)

    def value_step(r, carry):
        used = (live_of(r) + ch - 1) // ch
        for n in range(1, chunks + 1):

            @pl.when(used == n)
            def _():
                for c in range(n):
                    kv_copy(r, 1, c).wait()
                acc[r] = dot(wts[r, :, : n * ch], kv[r, 1, : n * ch, :])

        return carry

    lax.fori_loop(0, rows, value_step, 0)

    sink_part = dot(jnp.concatenate(sink_w, axis=0).astype(BF), sink_v[...])
    vf32 = vf.astype(F32)
    attended = []
    for r in range(rows):
        t = acc[r] + sink_part[r * ROWS : (r + 1) * ROWS, :] + fresh_w[r] * vf32[r : r + 1, :]
        attended.append(jnp.sum(jnp.where(head_mask, t, 0.0), axis=0, keepdims=True))
    attended = jnp.concatenate(attended, axis=0).astype(BF)
    ow_copy.wait()
    part[...] = dot(attended, ow_buf[...])


def attend(groups, heads_axis, fspan, lens, hidden, gain, bias, cos, sin, sk, sv, idx, rw, w, win, ow):
    rows, width = hidden.shape
    local = bias.shape[1]
    length = win.shape[2]
    chunks = 4 if length % 4 == 0 else 1
    span = rows + CAP * groups
    return pl.pallas_call(
        functools.partial(attend_kernel, groups, heads_axis),
        out_shape=(
            jax.ShapeDtypeStruct((rows, width), F32),
            jax.ShapeDtypeStruct((rows, local), BF),
            jax.ShapeDtypeStruct((rows, local), BF),
            jax.ShapeDtypeStruct((groups * span, groups * rows), BF),
            jax.ShapeDtypeStruct((3 * rows, groups * heads_axis * fspan), BF),
        ),
        in_specs=[SM] + [VM] * 9 + [HB] * 3,
        out_specs=(VM,) * 5,
        scratch_shapes=[
            pltpu.VMEM((3, width, local), BF),
            pltpu.VMEM((rows, 2, length, local), BF),
            pltpu.VMEM((local, width), BF),
            pltpu.VMEM((rows, ROWS, local), BF),
            pltpu.VMEM((rows, ROWS, length), F32),
            pltpu.VMEM((rows, ROWS, length), BF),
            pltpu.VMEM((rows, ROWS, local), F32),
            pltpu.SemaphoreType.DMA((3, 2)),
            pltpu.SemaphoreType.DMA((rows, 2, chunks)),
            pltpu.SemaphoreType.DMA(()),
        ],
        compiler_params=params(52 * MB),
        name="attend",
    )(lens, hidden, gain, bias, cos, sin, sk, sv, idx, rw, w, win, ow)


def dispatch_kernel(groups, summed, hidden, gain, gate_vec, big, send, gate_out, own_out, keep):
    rows, width = hidden.shape
    resid = hidden[...].astype(F32) + summed[...]
    keep[...] = resid
    ms = jnp.mean(resid * resid, axis=-1, keepdims=True)
    tokens = (resid * lax.rsqrt(ms + EPSILON) * gain[...]).astype(BF).astype(F32)
    gate = jax.nn.sigmoid(jnp.sum(tokens * gate_vec[...], axis=-1, keepdims=True))
    gate_out[...] = jnp.broadcast_to(gate, gate_out.shape)
    w = width // groups
    stacked = jnp.concatenate([tokens[:, j * w : (j + 1) * w] for j in range(groups)], axis=0)
    send[...] = dot(big[...], stacked.astype(BF)).astype(BF)
    slot = own_out.shape[1]
    start = pl.multiple_of(lax.axis_index("head") * slot, HD)
    own_out[...] = keep[:, pl.ds(start, slot)]


def dispatch(groups, slot, summed, hidden, gain, gate_vec, big):
    rows, width = hidden.shape
    return pl.pallas_call(
        functools.partial(dispatch_kernel, groups),
        out_shape=(
            jax.ShapeDtypeStruct((big.shape[0], width // groups), BF),
            jax.ShapeDtypeStruct((rows, HD), F32),
            jax.ShapeDtypeStruct((rows, slot), F32),
        ),
        in_specs=[VM] * 5,
        out_specs=(VM,) * 3,
        scratch_shapes=[pltpu.VMEM((rows, width), F32)],
        compiler_params=params(16 * MB),
        name="dispatch",
    )(summed, hidden, gain, gate_vec, big)


def shared_in_kernel(groups, rows, arrived, weights, out):
    span = arrived.shape[0] // groups
    x = jnp.concatenate(
        [arrived[g * span : g * span + rows, :] for g in range(groups)], axis=0
    )
    f = weights.shape[2]
    out[:, :f] = dot(x, weights[0]).astype(BF)
    out[:, f:] = dot(x, weights[1]).astype(BF)


def shared_in(groups, rows, arrived, weights):
    f = weights.shape[2]
    return pl.pallas_call(
        functools.partial(shared_in_kernel, groups, rows),
        out_shape=jax.ShapeDtypeStruct((groups * rows, 2 * f), BF),
        in_specs=[VM] * 2,
        out_specs=VM,
        compiler_params=params(16 * MB),
        name="shared_in",
    )(arrived, weights)


def shared_act_kernel(groups, sums, out):
    rows = sums.shape[0] // groups
    f = out.shape[1]
    total = sums[0:rows, :].astype(F32)
    for g in range(1, groups):
        total = total + sums[g * rows : (g + 1) * rows, :].astype(F32)
    gate, up = total[:, :f], total[:, f:]
    hidden = (jax.nn.silu(gate) * up).astype(BF)
    for g in range(groups):
        out[g * rows : (g + 1) * rows, :] = hidden


def shared_act(groups, sums):
    f = sums.shape[1] // 2
    return pl.pallas_call(
        functools.partial(shared_act_kernel, groups),
        out_shape=jax.ShapeDtypeStruct((sums.shape[0], f), BF),
        in_specs=[VM],
        out_specs=VM,
        compiler_params=params(16 * MB),
        name="shared_act",
    )(sums)


def expert_kernel(groups, rows, arrived, gu, down, out, xbuf, acc):
    step = pl.program_id(0)
    w = arrived.shape[1]
    slots = groups * CAP

    @pl.when(step == 0)
    def _():
        total = arrived.shape[0]
        span = total // groups
        line, lane = iota((groups * slots, total), 0), iota((groups * slots, total), 1)
        j, g, c = line // slots, line % slots // CAP, line % CAP
        pickm = one(lane == g * span + rows + j * CAP + c).astype(BF)
        x = dot(pickm, arrived[...])
        for jj in range(groups):
            xbuf[:, jj * w : (jj + 1) * w] = x[jj * slots : (jj + 1) * slots, :].astype(BF)
        acc[...] = jnp.zeros_like(acc)

    gate = lax.dot_general(xbuf[...], gu[0], NT, preferred_element_type=F32)
    up = lax.dot_general(xbuf[...], gu[1], NT, preferred_element_type=F32)
    hidden = (jax.nn.silu(gate) * up).astype(BF)
    acc[...] += dot(hidden, down[...])

    @pl.when(step == pl.num_programs(0) - 1)
    def _():
        for jj in range(groups):
            out[jj * slots : (jj + 1) * slots, :] = acc[:, jj * w : (jj + 1) * w].astype(BF)


def experts(groups, rows, arrived, gate_up, down):
    fe, width = down.shape
    piece = 352 if fe % 352 == 0 else fe
    slots = groups * CAP
    total, w = arrived.shape
    return pl.pallas_call(
        functools.partial(expert_kernel, groups, rows),
        out_shape=jax.ShapeDtypeStruct((groups * slots, w), BF),
        grid=(fe // piece,),
        in_specs=[
            pl.BlockSpec((total, w), lambda i: (0, 0)),
            pl.BlockSpec((2, piece, width), lambda i: (0, i, 0)),
            pl.BlockSpec((piece, width), lambda i: (i, 0)),
        ],
        out_specs=pl.BlockSpec((groups * slots, w), lambda i: (0, 0)),
        scratch_shapes=[pltpu.VMEM((slots, width), BF), pltpu.VMEM((slots, width), F32)],
        compiler_params=params(24 * MB, dimension_semantics=("arbitrary",)),
        cost_estimate=pl.CostEstimate(
            flops=6 * slots * fe * width, transcendentals=slots * fe, bytes_accessed=6 * fe * width
        ),
        name="experts",
    )(arrived, gate_up, down)


def give_back_kernel(groups, heads_axis, rows, shared_hidden, down, routed, out):
    shared = dot(shared_hidden[...], down[...]).astype(BF)
    both = jnp.concatenate([shared, routed[...]], axis=0)
    n_shared, n_all = shared.shape[0], both.shape[0]
    total = out.shape[0]
    fspan = total // (groups * heads_axis)
    ratio = groups // heads_axis
    line, lane = iota((total, n_all), 0), iota((total, n_all), 1)
    dev, t = line // fspan, line % fspan
    q, h = dev // heads_axis, dev % heads_axis
    mine = h == lax.axis_index("req") // ratio
    u = t - rows
    j = h * ratio + u % ratio
    target = jnp.where(
        t < rows,
        jnp.where(mine, q * rows + t, -1),
        jnp.where(u < CAP * ratio, n_shared + j * (groups * CAP) + q * CAP + u // ratio, -1),
    )
    out[...] = dot(one(target == lane).astype(BF), both).astype(BF)


def give_back(groups, heads_axis, rows, fspan, shared_hidden, down, routed):
    return pl.pallas_call(
        functools.partial(give_back_kernel, groups, heads_axis, rows),
        out_shape=jax.ShapeDtypeStruct((groups * heads_axis * fspan, down.shape[1]), BF),
        in_specs=[VM] * 3,
        out_specs=VM,
        compiler_params=params(16 * MB),
        name="give_back",
    )(shared_hidden, down, routed)


def finish_kernel(groups, heads_axis, returned, fin, gate, own, out):
    rows = own.shape[0]
    w = returned.shape[1]
    ratio = groups // heads_axis
    total = returned.shape[0]
    fspan = total // (groups * heads_axis)
    my_head = lax.axis_index("head")
    line, lane = iota((3 * rows, total), 0) % rows, iota((3 * rows, total), 1)
    q, t = lane // (fspan * heads_axis), lane % fspan
    gate3 = split3(gate[:, 0:1])
    base = fin[...].astype(F32)
    for p in range(ratio):
        routed_w = jnp.where((t - rows) % ratio == p, base, 0.0)
        shared_w = jnp.where((t == line) & (q == my_head * ratio + p), gate3, 0.0)
        weight = jnp.where(t < rows, shared_w, routed_w)
        terms = dot(weight.astype(BF), returned[...])
        value = terms[:rows] + terms[rows : 2 * rows] + terms[2 * rows :]
        out[:, p * w : (p + 1) * w] = (own[:, p * w : (p + 1) * w] + value).astype(BF)


def finish(groups, heads_axis, returned, fin, gate, own):
    return pl.pallas_call(
        functools.partial(finish_kernel, groups, heads_axis),
        out_shape=jax.ShapeDtypeStruct(own.shape, BF),
        in_specs=[VM] * 4,
        out_specs=VM,
        compiler_params=params(16 * MB),
        name="finish",
    )(returned, fin, gate, own)


def local(
    hidden_state,
    attend_gain,
    input_weight,
    input_bias,
    output_weight,
    window_cache,
    sink_cache,
    lengths,
    expert_index,
    router_weight,
    mixture_gain,
    expert_gate_up,
    expert_down,
    shared_gate_up,
    shared_down,
    shared_gate,
):
    rows, width = hidden_state.shape
    local_width = input_weight.shape[2]
    groups = lax.axis_size("req")
    heads_axis = lax.axis_size("head")
    slot = width // heads_axis
    fspan = 16

    half = HD // 2
    frequencies = F32(ROPE_BASE) ** (-(2.0 / HD) * jnp.arange(half).astype(F32))
    angles = lengths.astype(F32)[:, None] * frequencies[None, :]
    cosine, sine = jnp.cos(angles), jnp.sin(angles)
    cos = jnp.concatenate([cosine, cosine], axis=1)
    sin = jnp.concatenate([-sine, sine], axis=1)
    sink_k = sink_cache[:, 0].reshape(rows * SINKS, local_width)
    sink_v = sink_cache[:, 1].reshape(rows * SINKS, local_width)

    part, key, value, big, fin = attend(
        groups,
        heads_axis,
        fspan,
        lengths,
        hidden_state,
        attend_gain[None],
        input_bias,
        cos,
        sin,
        sink_k,
        sink_v,
        expert_index,
        router_weight,
        jnp.transpose(input_weight, (1, 0, 2)),
        window_cache,
        output_weight,
    )
    new_kv = jnp.stack([key, value], axis=1)
    summed = part
    bit = 1
    while bit < heads_axis:
        summed = summed + lax.ppermute(
            summed, "head", [(j, j ^ bit) for j in range(heads_axis)]
        )
        bit *= 2

    send, gate, own = dispatch(
        groups, slot, summed, hidden_state, mixture_gain[None], shared_gate[None], big
    )
    arrived = lax.all_to_all(send, "req", split_axis=0, concat_axis=0, tiled=True)
    sums = shared_in(groups, rows, arrived, shared_gate_up)
    sums = lax.all_to_all(sums, "req", split_axis=0, concat_axis=0, tiled=True)
    routed = experts(groups, rows, arrived, expert_gate_up, expert_down)
    shared_hidden = shared_act(groups, sums)
    shared_hidden = lax.all_to_all(shared_hidden, "req", split_axis=0, concat_axis=0, tiled=True)
    back = give_back(groups, heads_axis, rows, fspan, shared_hidden, shared_down, routed)
    returned = lax.all_to_all(back, ("req", "head"), split_axis=0, concat_axis=0, tiled=True)
    return finish(groups, heads_axis, returned, fin, gate, own), new_kv


def solution(mesh):
    return jax.shard_map(
        local,
        mesh=mesh,
        in_specs=(
            P("req", None),
            P(),
            P(None, None, "head"),
            P(None, "head"),
            P("head", None),
            P("req", None, None, "head"),
            P("req", None, None, "head"),
            P("req"),
            P("req", None),
            P("req", None),
            P(),
            P(None, ("req", "head"), None),
            P(("req", "head"), None),
            P(None, "req", "head"),
            P("head", "req"),
            P(),
        ),
        out_specs=(P("req", "head"), P("req", None, "head")),
        check_vma=False,
    )
```

time: 309 us -> 88.8 us (0.29)
  waiting for transfers between devices: 98.6 us -> 13.3 us
  local copies, waits for them, and re-layouts: 86.9 us -> 12.7 us
  matrix products: 39.7 us -> 0 us
  Pallas kernels: 0 us -> 21.3 us
  blocking collectives: 43.2 us -> 27.1 us
  other arithmetic: 14.9 us -> 0.88 us
  between operations: 14 us -> 0.76 us
  starting transfers between devices: 9.11 us -> 12.8 us
    psum x2 -> x0, waiting for transfers between devices: 78.1 us -> none  [the longest x1 57.6 us: local(): shared_terms = lax.psum(shared_terms, 'req')]
    another operation x3 -> x2, local copies, waits for them, and re-layouts: 46 us -> 0.03 us  [the longest x1 0.01 us: local(): sink_v = sink_cache[:, 1].reshape(rows * SINKS, local_width)]
    dot_general x14 -> x0, matrix products: 39.7 us -> none  [the longest x1 8.32 us: window_values(): jnp.einsum('rhs,rshd->rhd', kept_weights, value_rows, preferred_element_t...]
    all_gather x1 -> x0, blocking collectives: 32.8 us -> none  [local(): all_tokens = lax.all_gather(tokens, 'req', axis=0, tiled=True)]
    slice x1, local copies, waits for them, and re-layouts: 22.5 us -> 0.8 us  [local(): sink_v = sink_cache[:, 1].reshape(rows * SINKS, local_width)]
    pallas_call x0 -> x7, Pallas kernels: none -> 21.3 us  [the longest x1 12.3 us: attend(): pl.pallas_call(functools.partial(attend_kernel, groups, heads_axis), out_...]
    all_to_all x1 -> x2, blocking collectives: 10.4 us -> 27.1 us  [the longest x1 15.1 us: local(): lax.all_to_all(send, 'req', split_axis=0, concat_axis=0, tiled=True)]
    reduce_scatter x1 -> x0, waiting for transfers between devices: 15.7 us -> none  [local(): final = lax.psum_scatter(routed, 'head', scatter_dimension=1, tiled=True)]
  transfers between devices with their start and end apart: 5 -> 4, of which waited for: 4 -> 3; matrix products, arithmetic and copies ran while one was open for 10% -> 1% of each run, Pallas kernels for 0% -> 6%
where the time goes in v1:
time: 88.8 us
  blocking collectives  27.1 us (31%)
  Pallas kernels  21.3 us (24%)
  waiting for transfers between devices  13.3 us (15%)
  starting transfers between devices  12.8 us (14%)
  local copies, waits for them, and re-layouts  12.7 us (14%)
    all_to_all x1, blocking collectives, local(): lax.all_to_all(send, 'req', split_axis=0, concat_axis=0, tiled=True)  15.1 us
    pallas_call x1, Pallas kernels, attend(): pl.pallas_call(functools.partial(attend_kernel, groups, heads_axis), out_...  12.3 us
    all_to_all x1, blocking collectives, local(): sums = lax.all_to_all(sums, 'req', split_axis=0, concat_axis=0, tiled=True)  12 us
    unnamed x23, local copies, waits for them, and re-layouts  11.9 us
    all_to_all x1, waiting for transfers between devices, local(): lax.all_to_all(back, ('req', 'head'), split_axis=0, concat_axis=0, tiled=...  9.97 us
    all_to_all x1, starting transfers between devices, local(): lax.all_to_all(back, ('req', 'head'), split_axis=0, concat_axis=0, tiled=...  5.98 us
    pallas_call x1, Pallas kernels, experts(): pl.pallas_call(functools.partial(expert_kernel, groups, rows), out_shape=...  5.51 us
    ppermute x2, starting transfers between devices, local(): lax.ppermute(summed, 'head', [(j, j ^ bit) for j in range(heads_axis)])  3.45 us
  transfers between devices with their start and end apart: 4, of which 3 were waited for; matrix products, arithmetic and copies ran while one was open for 1% of the time, Pallas kernels for 6%

profile of v1, /device:TPU:0, one launch (start us, length us, event | category | flops | bytes accessed | tf_op | source)
XLA Modules:
  0.0 88.8 jit_solution(4995018817570544727)
XLA Ops:
  0.6 0.7 convert_element_type.10
  1.3 0.8 copy.18.idx
  2.1 0.8 copy.19.rw
  2.8 0.8 fusion.1
  3.7 0.1 fusion
  3.8 0.1 pad_maximum_fusion.1
  3.8 0.0 copy-start.4
  3.8 0.8 copy-done.4
  4.6 0.0 copy-start.7
  4.6 0.7 copy-done.7
  5.3 0.0 copy-start.8
  5.3 0.7 copy-done.8
  6.0 0.0 copy-start.9
  6.0 0.7 copy-done.9
  6.7 0.0 copy-start.5
  6.7 0.0 copy-start.6
  6.7 0.0 copy-start.2
  6.7 12.3 %attend.1 = (f32[8,2048]{1,0:T(8,128)S(1)}, bf16[8,512]{1,0:T(8,128)(2,1)S(1)}, bf16[8,512]{1,0:T(8,128)(2,1)S(1)}, bf16[192,64]{1,0:T(8,128)(2,1)S(1)}, bf16[24,512]{1,0:T(8,128)(2,1)S(1)}) custom-call(s32[8]{0:T(128)S(1)} %copy-done.9, bf16[8,2048]{1,0:T(8,128)(2,1)S(1)} %copy-done.4, f32[1,2048]{1,0:T(1,128)S(1)} %bitcast.25, f32[3,512]{1,0:T(4,128)S(1)} %copy-done.8, ...), custom_call_target="tpu_custom_call" | custom-call | tf_op jit(solution)/shard_map/attend/pallas_call | solution.py:278
  19.0 0.5 collective-permute-start
  19.5 0.9 %collective-permute-done = f32[8,2048]{1,0:T(8,128)S(1)} collective-permute-done((f32[8,2048]{1,0:T(8,128)S(1)}, f32[8,2048]{1,0:T(8,128)S(1)}, u32[]{:S(2)}, u32[]{:S(2)}) %collective-permute-start) | collective-permute-done | bytes 65568 | tf_op jit(solution)/shard_map/ppermute | solution.py:556
  20.4 2.9 %collective-permute-start.1 = (f32[8,2048]{1,0:T(8,128)S(1)}, f32[8,2048]{1,0:T(8,128)S(1)}, u32[]{:S(2)}, u32[]{:S(2)}) collective-permute-start(f32[8,2048]{1,0:T(8,128)S(1)} %add.6), channel_id=1, source_target_pairs={{0,2},{1,3},{2,0},{3,1},{4,6},{5,7},{6,4},{7,5},{8,10},{9,11},{10,... | collective-permute-start | bytes 196616 | tf_op jit(solution)/shard_map/ppermute | solution.py:556
  23.3 2.4 %collective-permute-done.1 = f32[8,2048]{1,0:T(8,128)S(1)} collective-permute-done((f32[8,2048]{1,0:T(8,128)S(1)}, f32[8,2048]{1,0:T(8,128)S(1)}, u32[]{:S(2)}, u32[]{:S(2)}) %collective-permute-start.1) | collective-permute-done | bytes 65568 | tf_op jit(solution)/shard_map/ppermute | solution.py:556
  25.8 0.0 copy-done.5
  25.8 0.0 copy-done.6
  25.8 0.3 dispatch.1
  26.0 15.1 %all_to_all.44 = bf16[8,24,256]{2,1,0:T(8,128)(2,1)S(1)} all-to-all(bf16[8,24,256]{2,1,0:T(8,128)(2,1)S(1)} %bitcast.20), channel_id=1, replica_groups=mesh['req'=8,'head'=4] {'req'}, dimensions={0} | all-to-all | bytes 196608 | tf_op jit(solution)/shard_map/all_to_all | solution.py:564
  41.2 0.0 copy-done.2
  41.2 0.3 shared_in.1
  41.5 12.0 %all_to_all.45 = bf16[8,8,2816]{2,1,0:T(8,128)(2,1)S(1)} all-to-all(bf16[8,8,2816]{2,1,0:T(8,128)(2,1)S(1)} %bitcast.15), channel_id=1, replica_groups=mesh['req'=8,'head'=4] {'req'}, dimensions={0} | all-to-all | bytes 720896 | tf_op jit(solution)/shard_map/all_to_all | solution.py:566
  53.5 0.7 shared_act.1
  54.2 3.4 %all-to-all-start.2 = ((bf16[8,8,1408]{2,1,0:T(8,128)(2,1)}), bf16[8,8,1408]{2,1,0:T(8,128)(2,1)S(1)}, u32[]{:S(2)}, u32[]{:S(2)}) async-start(bf16[8,8,1408]{2,1,0:T(8,128)(2,1)} %bitcast.8), calls=%async_computation.2 | async-start | bytes 360448 | tf_op jit(solution)/shard_map/all_to_all | solution.py:569
  57.6 0.0 copy-start
  57.6 4.3 %copy-done = bf16[2,1408,2048]{2,1,0:T(8,128)(2,1)S(1)} copy-done((bf16[2,1408,2048]{2,1,0:T(8,128)(2,1)S(1)}, bf16[2,1408,2048]{2,1,0:T(8,128)(2,1)}, u32[]{:S(2)}) %copy-start) | copy-done | bytes 11534360
  61.9 0.0 copy-start.1
  61.9 2.6 %copy-done.1 = bf16[1408,2048]{1,0:T(8,128)(2,1)S(1)} copy-done((bf16[1408,2048]{1,0:T(8,128)(2,1)S(1)}, bf16[1408,2048]{1,0:T(8,128)(2,1)}, u32[]{:S(2)}) %copy-start.1) | copy-done | bytes 5767192
  64.5 0.0 copy-start.3
  64.5 5.5 %experts.1.routed = bf16[128,256]{1,0:T(8,128)(2,1)S(1)} custom-call(bf16[192,256]{1,0:T(8,128)(2,1)S(1)} %bitcast.18, bf16[2,1408,2048]{2,1,0:T(8,128)(2,1)S(1)} %copy-done, bf16[1408,2048]{1,0:T(8,128)(2,1)S(1)} %copy-done.1), custom_call_target="tpu_custom_call" | custom-call | flops 276824064 | bytes 17301504 | tf_op jit(solution)/shard_map/experts/pallas_call | solution.py:418
  70.0 0.0 all-to-all-done.2
  70.1 0.0 copy-done.3
  70.1 1.3 %give_back.1 = bf16[512,256]{1,0:T(8,128)(2,1)} custom-call(bf16[64,1408]{1,0:T(8,128)(2,1)S(1)} %bitcast.19, bf16[1408,256]{1,0:T(8,128)(2,1)S(1)} %copy-done.3, bf16[128,256]{1,0:T(8,128)(2,1)S(1)} %experts.1.routed), custom_call_target="tpu_custom_call" | custom-call | tf_op jit(solution)/shard_map/give_back/pallas_call | solution.py:459
  71.4 6.0 %all-to-all-start.3 = ((bf16[32,16,256]{2,1,0:T(8,128)(2,1)}), bf16[32,16,256]{2,1,0:T(8,128)(2,1)S(1)}, u32[]{:S(2)}, u32[]{:S(2)}) async-start(bf16[32,16,256]{2,1,0:T(8,128)(2,1)} %bitcast.10), calls=%async_computation.3 | async-start | bytes 524288 | tf_op jit(solution)/shard_map/all_to_all | solution.py:571
  77.4 0.6 copy.20
  78.0 10.0 %all-to-all-done.3 = bf16[32,16,256]{2,1,0:T(8,128)(2,1)S(1)} async-done(((bf16[32,16,256]{2,1,0:T(8,128)(2,1)}), bf16[32,16,256]{2,1,0:T(8,128)(2,1)S(1)}, u32[]{:S(2)}, u32[]{:S(2)}) %all-to-all-start.3) | async-done | bytes 262176 | tf_op jit(solution)/shard_map/all_to_all | solution.py:571
  87.9 0.8 finish.1
  (6 shorter events, 0.1 us)
Async XLA Ops:
  3.8 0.8 copy-start.4
  4.6 0.7 copy-start.7
  5.3 0.7 copy-start.8
  6.0 0.7 copy-start.9
  6.7 19.1 %copy-start.5 = (f32[2048]{0:T(1024)S(1)}, f32[2048]{0:T(1024)}, u32[]{:S(2)}) copy-start(f32[2048]{0:T(1024)} %param.26) | copy-start | bytes 24580
  6.7 19.1 %copy-start.6 = (f32[2048]{0:T(1024)S(1)}, f32[2048]{0:T(1024)}, u32[]{:S(2)}) copy-start(f32[2048]{0:T(1024)} %param.31) | copy-start | bytes 24580
  6.7 34.5 %copy-start.2 = (bf16[2,256,1408]{2,1,0:T(8,128)(2,1)S(1)}, bf16[2,256,1408]{2,1,0:T(8,128)(2,1)}, u32[]{:S(2)}) copy-start(bf16[2,256,1408]{2,1,0:T(8,128)(2,1)} %weights.1) | copy-start | bytes 4325380
  19.0 1.4 %collective-permute-start = (f32[8,2048]{1,0:T(8,128)S(1)}, f32[8,2048]{1,0:T(8,128)S(1)}, u32[]{:S(2)}, u32[]{:S(2)}) collective-permute-start(f32[8,2048]{1,0:T(8,128)S(1)} %get-tuple-element.10), channel_id=1, source_target_pairs={{0,1},{1,0},{2,3},{3,2},{4,5},{5,4},{6,7},{7,6},{8,9},{9,8},{10,11... | collective-permute-start | bytes 196616 | tf_op jit(solution)/shard_map/ppermute | solution.py:556
  20.4 5.3 %collective-permute-start.1 = (f32[8,2048]{1,0:T(8,128)S(1)}, f32[8,2048]{1,0:T(8,128)S(1)}, u32[]{:S(2)}, u32[]{:S(2)}) collective-permute-start(f32[8,2048]{1,0:T(8,128)S(1)} %add.6), channel_id=1, source_target_pairs={{0,2},{1,3},{2,0},{3,1},{4,6},{5,7},{6,4},{7,5},{8,10},{9,11},{10,... | collective-permute-start | bytes 196616 | tf_op jit(solution)/shard_map/ppermute | solution.py:556
  54.2 15.8 %all-to-all-start.2 = ((bf16[8,8,1408]{2,1,0:T(8,128)(2,1)}), bf16[8,8,1408]{2,1,0:T(8,128)(2,1)S(1)}, u32[]{:S(2)}, u32[]{:S(2)}) async-start(bf16[8,8,1408]{2,1,0:T(8,128)(2,1)} %bitcast.8), calls=%async_computation.2 | async-start | bytes 360448 | tf_op jit(solution)/shard_map/all_to_all | solution.py:569
  57.6 4.3 %copy-start = (bf16[2,1408,2048]{2,1,0:T(8,128)(2,1)S(1)}, bf16[2,1408,2048]{2,1,0:T(8,128)(2,1)}, u32[]{:S(2)}) copy-start(bf16[2,1408,2048]{2,1,0:T(8,128)(2,1)} %gu.1) | copy-start | bytes 34603012
  61.9 2.6 %copy-start.1 = (bf16[1408,2048]{1,0:T(8,128)(2,1)S(1)}, bf16[1408,2048]{1,0:T(8,128)(2,1)}, u32[]{:S(2)}) copy-start(bf16[1408,2048]{1,0:T(8,128)(2,1)} %down.2) | copy-start | bytes 17301508
  64.5 5.5 %copy-start.3 = (bf16[1408,256]{1,0:T(8,128)(2,1)S(1)}, bf16[1408,256]{1,0:T(8,128)(2,1)}, u32[]{:S(2)}) copy-start(bf16[1408,256]{1,0:T(8,128)(2,1)} %down.3) | copy-start | bytes 2162692
  71.4 16.6 %all-to-all-start.3 = ((bf16[32,16,256]{2,1,0:T(8,128)(2,1)}), bf16[32,16,256]{2,1,0:T(8,128)(2,1)S(1)}, u32[]{:S(2)}, u32[]{:S(2)}) async-start(bf16[32,16,256]{2,1,0:T(8,128)(2,1)} %bitcast.10), calls=%async_computation.3 | async-start | bytes 524288 | tf_op jit(solution)/shard_map/all_to_all | solution.py:571

commit v2 on v1

v2 whole, which is shorter than its diff:
```python
import functools
import math

import jax
import jax.numpy as jnp
from jax import lax
from jax.experimental import pallas as pl
from jax.experimental.pallas import tpu as pltpu
from jax.sharding import PartitionSpec as P

HD = 128
EXPERTS = 32
FE = 1408
SINKS = 4
CAP = 2
ROWS = 8

EPSILON = 1e-06
ROPE_BASE = 1000000.0
MB = 1 << 20
BF = jnp.bfloat16
F32 = jnp.float32


def stay(x):
    return pltpu.with_memory_space_constraint(x, pltpu.HBM)


NT = (((1,), (1,)), ((), ()))


def iota(shape, dim):
    return lax.broadcasted_iota(jnp.int32, shape, dim)


def one(cond):
    return jnp.where(cond, 1.0, 0.0).astype(F32)


def dot(a, b):
    return jnp.dot(a, b, preferred_element_type=F32)


def split3(x):
    hi = x.astype(BF).astype(F32)
    mid = (x - hi).astype(BF).astype(F32)
    lo = (x - hi - mid).astype(BF).astype(F32)
    return hi, mid, lo


def params(limit, **kw):
    return pltpu.CompilerParams(vmem_limit_bytes=limit, **kw)


VM = pl.BlockSpec(memory_space=pltpu.VMEM)
SM = pl.BlockSpec(memory_space=pltpu.SMEM)
HB = pl.BlockSpec(memory_space=pltpu.HBM)


def routing_tables(groups, heads_axis, idx, rw, big_out, meta_out):
    rows = idx.shape[1]
    local_experts = EXPERTS // groups
    pick = lax.axis_index("head") // (heads_axis // local_experts)
    hit = jnp.zeros((EXPERTS, rows), F32)
    comb = jnp.zeros((EXPERTS, rows), F32)
    line_e = iota((EXPERTS, rows), 0)
    for k in range(idx.shape[0]):
        eq = one(idx[k : k + 1, :] == line_e)
        hit = hit + eq
        comb = comb + eq * rw[k : k + 1, :]
    above = one(iota((rows, rows), 0) < iota((rows, rows), 1))
    rank = dot(hit.astype(BF), above.astype(BF))
    sel = [hit * one(rank == c) for c in range(CAP)]
    span = rows + CAP * groups
    total = groups * span
    row_g = iota((total, EXPERTS), 0) // span
    row_t = iota((total, EXPERTS), 0) % span
    mine = iota((total, EXPERTS), 1) == row_g * local_experts + pick
    z = jnp.zeros((total, rows), F32)
    for c in range(CAP):
        pickc = mine & (row_t >= rows) & ((row_t - rows) % CAP == c)
        z = z + dot(one(pickc).astype(BF), sel[c].astype(BF))
    nb = groups * rows
    rep = one(iota((rows, nb), 0) == iota((rows, nb), 1) % rows)
    zz = dot(z.astype(BF), rep.astype(BF))
    g2 = iota((total, nb), 0) // span
    t2 = iota((total, nb), 0) % span
    j2 = iota((total, nb), 1) // rows
    r2 = iota((total, nb), 1) % rows
    direct = one((j2 == g2) & (r2 == t2))
    placed = zz * one(j2 == (t2 - rows) // CAP)
    big_out[...] = jnp.where(t2 < rows, direct, placed).astype(BF)

    w = meta_out.shape[1]
    again = one(iota((nb, rows), 0) % rows == iota((nb, rows), 1)).astype(BF)
    keep = iota((nb, EXPERTS), 1) == (iota((nb, EXPERTS), 0) // rows) * local_experts + pick
    meta = jnp.zeros((nb, w), F32)
    for c in range(CAP):
        for p, term in enumerate(split3(comb * sel[c])):
            wide = lax.dot_general(again, term.astype(BF), NT, preferred_element_type=F32)
            wide = jnp.where(keep, wide, 0.0).astype(BF)
            column = one(iota((EXPERTS, w), 1) == 3 * c + p).astype(BF)
            meta = meta + dot(wide, column)
    meta_out[...] = meta.astype(BF)


def attend_kernel(
    groups,
    heads_axis,
    freq,
    lens_hbm,
    hidden_hbm,
    gain_hbm,
    bias_hbm,
    sink_hbm,
    idx_hbm,
    rw_hbm,
    w_hbm,
    win_hbm,
    ow_hbm,
    part,
    key_out,
    value_out,
    big_out,
    meta_out,
    lens,
    hidden,
    gain,
    bias,
    sink,
    idx,
    rw,
    w_buf,
    kv,
    ow_buf,
    qbd,
    sc,
    wts,
    acc,
    small_sem,
    w_sem,
    kv_sem,
    ow_sem,
):
    rows, width = hidden.shape
    local = bias.shape[1]
    length = kv.shape[2]
    chunks = kv_sem.shape[2]
    ch = length // chunks
    halves = w_sem.shape[1]
    wc = width // halves

    small = [
        pltpu.make_async_copy(src, dst, small_sem.at[i])
        for i, (src, dst) in enumerate(
            (
                (lens_hbm, lens),
                (hidden_hbm, hidden),
                (gain_hbm, gain),
                (bias_hbm, bias),
                (idx_hbm, idx),
                (rw_hbm, rw),
                (sink_hbm, sink),
            )
        )
    ]

    def w_copy(c, i):
        return pltpu.make_async_copy(
            w_hbm.at[c, pl.ds(i * wc, wc)], w_buf.at[c, pl.ds(i * wc, wc)], w_sem.at[c, i]
        )

    def kv_copy(r, t, c):
        return pltpu.make_async_copy(
            win_hbm.at[r, t, pl.ds(c * ch, ch)], kv.at[r, t, pl.ds(c * ch, ch)], kv_sem.at[r, t, c]
        )

    def live_of(r):
        return jnp.minimum(lens[r] - SINKS + 1, length)

    def fetch(t):
        def step(r, carry):
            live = live_of(r)
            for c in range(chunks):

                @pl.when(c * ch < live)
                def _():
                    kv_copy(r, t, c).start()

            return carry

        lax.fori_loop(0, rows, step, 0)

    for copy in small:
        copy.start()
    for c in range(3):
        for i in range(halves):
            w_copy(c, i).start()
    small[0].wait()
    fetch(0)
    fetch(1)
    ow_copy = pltpu.make_async_copy(ow_hbm, ow_buf, ow_sem)
    ow_copy.start()
    for copy in small[1:]:
        copy.wait()

    routing_tables(groups, heads_axis, idx, rw, big_out, meta_out)

    place = jnp.concatenate([jnp.full((1, HD // 2), lens[r], jnp.int32) for r in range(rows)], axis=0)
    angles = place.astype(F32) * freq[...]
    cosine, sine = jnp.cos(angles), jnp.sin(angles)
    cos = jnp.concatenate([cosine, cosine], axis=1)
    sin = jnp.concatenate([-sine, sine], axis=1)

    x = hidden[...].astype(F32)
    ms = jnp.mean(x * x, axis=-1, keepdims=True)
    normed = (x * lax.rsqrt(ms + EPSILON) * gain[...]).astype(BF)
    proj = []
    for c in range(3):
        total_c = bias[c : c + 1, :]
        for i in range(halves):
            w_copy(c, i).wait()
            total_c = total_c + dot(
                normed[:, i * wc : (i + 1) * wc], w_buf[c, i * wc : (i + 1) * wc, :]
            )
        proj.append(total_c)

    def rotate(v):
        outs = []
        for h in range(local // HD):
            part_h = v[:, h * HD : (h + 1) * HD]
            outs.append(part_h * cos + pltpu.roll(part_h, HD // 2, 1) * sin)
        return jnp.concatenate(outs, axis=1)

    q = rotate(proj[0]).astype(BF).astype(F32)
    kf = rotate(proj[1]).astype(BF)
    vf = proj[2].astype(BF)
    key_out[...] = kf
    value_out[...] = vf
    head_mask = iota((ROWS, local), 1) // HD == iota((ROWS, local), 0)
    q3 = jnp.where(head_mask[None], q[:, None, :], 0.0)
    qbd[...] = q3.astype(BF)
    fresh_scores = jnp.sum(q3 * kf.astype(F32)[:, None, :], axis=-1, keepdims=True)

    sink_s = [
        lax.dot_general(qbd[r], sink[r, 0], NT, preferred_element_type=F32) / math.sqrt(HD)
        for r in range(rows)
    ]

    def score_step(r, carry):
        used = (live_of(r) + ch - 1) // ch
        for n in range(1, chunks + 1):

            @pl.when(used == n)
            def _():
                for c in range(n):
                    kv_copy(r, 0, c).wait()
                sc[r, :, : n * ch] = lax.dot_general(
                    qbd[r], kv[r, 0, : n * ch, :], NT, preferred_element_type=F32
                )

        return carry

    lax.fori_loop(0, rows, score_step, 0)

    pos = iota((ROWS, length), 1)
    rest = []
    vf32 = vf.astype(F32)
    for r in range(rows):
        slot = lax.rem(lens[r] - SINKS, length)
        is_fresh = pos == slot
        s = jnp.where(is_fresh, fresh_scores[r], sc[r]) / math.sqrt(HD)
        s = jnp.where(pos < live_of(r), s, -jnp.inf)
        ss = sink_s[r]
        top = jnp.maximum(
            jnp.max(s, axis=-1, keepdims=True), jnp.max(ss, axis=-1, keepdims=True)
        )
        e = jnp.exp(s - top)
        es = jnp.exp(ss - top)
        tot = jnp.sum(e, axis=-1, keepdims=True) + jnp.sum(es, axis=-1, keepdims=True)
        w = (e / tot).astype(BF).astype(F32)
        fresh_w = jnp.sum(jnp.where(is_fresh, w, 0.0), axis=-1, keepdims=True)
        rest.append(fresh_w * vf32[r : r + 1, :] + dot((es / tot).astype(BF), sink[r, 1]))
        wts[r] = jnp.where(is_fresh, 0.0, w).astype(BF)

    def value_step(r, carry):
        used = (live_of(r) + ch - 1) // ch
        for n in range(1, chunks + 1):

            @pl.when(used == n)
            def _():
                for c in range(n):
                    kv_copy(r, 1, c).wait()
                acc[r] = dot(wts[r, :, : n * ch], kv[r, 1, : n * ch, :])

        return carry

    lax.fori_loop(0, rows, value_step, 0)

    attended = [
        jnp.sum(jnp.where(head_mask, acc[r] + rest[r], 0.0), axis=0, keepdims=True)
        for r in range(rows)
    ]
    attended = jnp.concatenate(attended, axis=0).astype(BF)
    ow_copy.wait()
    part[...] = dot(attended, ow_buf[...])


def attend(groups, heads_axis, freq, lens, hidden, gain, bias, sink, idx, rw, w, win, ow):
    rows, width = hidden.shape
    local = bias.shape[1]
    length = win.shape[2]
    chunks = 4 if length % 4 == 0 else 1
    span = rows + CAP * groups
    return pl.pallas_call(
        functools.partial(attend_kernel, groups, heads_axis),
        out_shape=(
            jax.ShapeDtypeStruct((rows, width), F32),
            jax.ShapeDtypeStruct((rows, local), BF),
            jax.ShapeDtypeStruct((rows, local), BF),
            jax.ShapeDtypeStruct((groups * span, groups * rows), BF),
            jax.ShapeDtypeStruct((groups * rows, width // groups), BF),
        ),
        in_specs=[VM] + [HB] * 10,
        out_specs=(VM,) * 5,
        scratch_shapes=[
            pltpu.SMEM(lens.shape, lens.dtype),
            pltpu.VMEM(hidden.shape, hidden.dtype),
            pltpu.VMEM(gain.shape, gain.dtype),
            pltpu.VMEM(bias.shape, bias.dtype),
            pltpu.VMEM(sink.shape, sink.dtype),
            pltpu.VMEM(idx.shape, idx.dtype),
            pltpu.VMEM(rw.shape, rw.dtype),
            pltpu.VMEM((3, width, local), BF),
            pltpu.VMEM((rows, 2, length, local), BF),
            pltpu.VMEM((local, width), BF),
            pltpu.VMEM((rows, ROWS, local), BF),
            pltpu.VMEM((rows, ROWS, length), F32),
            pltpu.VMEM((rows, ROWS, length), BF),
            pltpu.VMEM((rows, ROWS, local), F32),
            pltpu.SemaphoreType.DMA((7,)),
            pltpu.SemaphoreType.DMA((3, 2)),
            pltpu.SemaphoreType.DMA((rows, 2, chunks)),
            pltpu.SemaphoreType.DMA(()),
        ],
        compiler_params=params(52 * MB),
        name="attend",
    )(freq, *map(stay, (lens, hidden, gain, bias, sink, idx, rw, w, win, ow)))


def dispatch_kernel(groups, summed, hidden, gain, gate_vec, big, meta, send, own_out, keep):
    rows, width = hidden.shape
    resid = hidden[...].astype(F32) + summed[...]
    keep[...] = resid
    ms = jnp.mean(resid * resid, axis=-1, keepdims=True)
    tokens = (resid * lax.rsqrt(ms + EPSILON) * gain[...]).astype(BF).astype(F32)
    gate = jax.nn.sigmoid(jnp.sum(tokens * gate_vec[...], axis=-1, keepdims=True))
    w = width // groups
    stacked = jnp.concatenate([tokens[:, j * w : (j + 1) * w] for j in range(groups)], axis=0)
    placed = dot(big[...], stacked.astype(BF)).astype(BF)
    lane = iota((rows, w), 1)
    extra = jnp.zeros((rows, w), F32)
    for p, term in enumerate(split3(gate)):
        extra = extra + jnp.where(lane == 3 * CAP + p, term, 0.0)
    span = placed.shape[0] // groups
    full = send.shape[0] // groups
    for g in range(groups):
        send[g * full : g * full + span, :] = placed[g * span : (g + 1) * span, :]
        told = meta[g * rows : (g + 1) * rows, :].astype(F32) + extra
        send[g * full + span : (g + 1) * full, :] = told.astype(BF)
    slot = own_out.shape[1]
    start = pl.multiple_of(lax.axis_index("head") * slot, HD)
    own_out[...] = keep[:, pl.ds(start, slot)]


def dispatch(groups, slot, summed, hidden, gain, gate_vec, big, meta):
    rows, width = hidden.shape
    return pl.pallas_call(
        functools.partial(dispatch_kernel, groups),
        out_shape=(
            jax.ShapeDtypeStruct((big.shape[0] + groups * rows, width // groups), BF),
            jax.ShapeDtypeStruct((rows, slot), F32),
        ),
        in_specs=[VM] * 6,
        out_specs=(VM,) * 2,
        scratch_shapes=[pltpu.VMEM((rows, width), F32)],
        compiler_params=params(16 * MB),
        name="dispatch",
    )(summed, hidden, gain, gate_vec, big, meta)


def shared_in_kernel(groups, rows, arrived, weights, out):
    span = arrived.shape[0] // groups
    x = jnp.concatenate(
        [arrived[g * span : g * span + rows, :] for g in range(groups)], axis=0
    )
    tokens = x.shape[0]
    both = jnp.concatenate([dot(x, weights[0]), dot(x, weights[1])], axis=0)
    out[...] = both.T.astype(BF)


def shared_in(groups, rows, arrived, weights):
    return pl.pallas_call(
        functools.partial(shared_in_kernel, groups, rows),
        out_shape=jax.ShapeDtypeStruct((weights.shape[2], 2 * groups * rows), BF),
        in_specs=[VM] * 2,
        out_specs=VM,
        compiler_params=params(16 * MB),
        name="shared_in",
    )(arrived, weights)


def expert_kernel(groups, rows, arrived, gu_hbm, down_hbm, out, gu, down, gu_sem, down_sem):
    pieces = down_sem.shape[0]
    piece = down.shape[0] // pieces

    def gu_copy(t, i):
        at = pl.ds(i * piece, piece)
        return pltpu.make_async_copy(gu_hbm.at[t, at], gu.at[t, at], gu_sem.at[t, i])

    def down_copy(i):
        at = pl.ds(i * piece, piece)
        return pltpu.make_async_copy(down_hbm.at[at], down.at[at], down_sem.at[i])

    for i in range(pieces):
        gu_copy(0, i).start()
        gu_copy(1, i).start()
        down_copy(i).start()

    slots = groups * CAP
    total = arrived.shape[0]
    span = total // groups
    line, lane = iota((groups * slots, total), 0), iota((groups * slots, total), 1)
    j, g, c = line // slots, line % slots // CAP, line % CAP
    pickm = one(lane == g * span + rows + j * CAP + c).astype(BF)
    x = dot(pickm, arrived[...])
    x = jnp.concatenate(
        [x[jj * slots : (jj + 1) * slots, :] for jj in range(groups)], axis=1
    ).astype(BF)
    result = jnp.zeros((slots, down.shape[1]), F32)
    for i in range(pieces):
        at = slice(i * piece, (i + 1) * piece)
        gu_copy(0, i).wait()
        gate = lax.dot_general(x, gu[0, at, :], NT, preferred_element_type=F32)
        gu_copy(1, i).wait()
        up = lax.dot_general(x, gu[1, at, :], NT, preferred_element_type=F32)
        hidden = (jax.nn.silu(gate) * up).astype(BF)
        down_copy(i).wait()
        result = result + dot(hidden, down[at, :])
    out[...] = result


def experts(groups, rows, arrived, gate_up, down):
    fe, width = down.shape
    pieces = fe // 352 if fe % 352 == 0 else 1
    slots = groups * CAP
    return pl.pallas_call(
        functools.partial(expert_kernel, groups, rows),
        out_shape=jax.ShapeDtypeStruct((slots, width), F32),
        in_specs=[VM, HB, HB],
        out_specs=VM,
        scratch_shapes=[
            pltpu.VMEM(gate_up.shape, BF),
            pltpu.VMEM(down.shape, BF),
            pltpu.SemaphoreType.DMA((2, pieces)),
            pltpu.SemaphoreType.DMA((pieces,)),
        ],
        compiler_params=params(32 * MB),
        cost_estimate=pl.CostEstimate(
            flops=6 * slots * fe * width, transcendentals=slots * fe, bytes_accessed=6 * fe * width
        ),
        name="experts",
    )(arrived, stay(gate_up), stay(down))


def give_back_kernel(groups, heads_axis, rows, sums, down, routed, arrived, out):
    total = sums[0].astype(F32)
    for g in range(1, groups):
        total = total + sums[g].astype(F32)
    tokens = groups * rows
    hidden = jax.nn.silu(total) * pltpu.roll(total, tokens, 1)
    hidden = hidden[:, :tokens].T.astype(BF)
    span = arrived.shape[0] // groups
    told = jnp.concatenate(
        [arrived[(g + 1) * span - rows : (g + 1) * span, :HD] for g in range(groups)], axis=0
    ).astype(F32)

    def column(k):
        return told[:, 3 * k : 3 * k + 1] + told[:, 3 * k + 1 : 3 * k + 2] + told[:, 3 * k + 2 : 3 * k + 3]

    gate = column(CAP)
    weight = [column(c) for c in range(CAP)]
    w = down.shape[2]
    ratio = groups // heads_axis
    for j in range(groups):
        shared = gate * dot(hidden, down[j])
        h, half = j // ratio, j % ratio
        for g in range(groups):
            at = slice(g * rows, (g + 1) * rows)
            value = shared[at]
            for c in range(CAP):
                line = routed[g * CAP + c : g * CAP + c + 1, j * w : (j + 1) * w]
                value = value + weight[c][at] * line
            to = (g * heads_axis + h) * rows
            out[to : to + rows, half * w : (half + 1) * w] = value.astype(BF)


def give_back(groups, heads_axis, rows, sums, down, routed, arrived):
    return pl.pallas_call(
        functools.partial(give_back_kernel, groups, heads_axis, rows),
        out_shape=jax.ShapeDtypeStruct(
            (groups * heads_axis * rows, routed.shape[1] // heads_axis), BF
        ),
        in_specs=[VM] * 4,
        out_specs=VM,
        compiler_params=params(16 * MB),
        name="give_back",
    )(sums, down, routed, arrived)


def finish_kernel(returned, own, out):
    rows = own.shape[0]
    total = own[...]
    for i in range(returned.shape[0] // rows):
        total = total + returned[i * rows : (i + 1) * rows, :].astype(F32)
    out[...] = total.astype(BF)


def finish(returned, own):
    return pl.pallas_call(
        finish_kernel,
        out_shape=jax.ShapeDtypeStruct(own.shape, BF),
        in_specs=[VM] * 2,
        out_specs=VM,
        compiler_params=params(16 * MB),
        name="finish",
    )(returned, own)


def local(
    hidden_state,
    attend_gain,
    input_weight,
    input_bias,
    output_weight,
    window_cache,
    sink_cache,
    lengths,
    expert_index,
    router_weight,
    mixture_gain,
    expert_gate_up,
    expert_down,
    shared_gate_up,
    shared_down,
    shared_gate,
):
    rows, width = hidden_state.shape
    local_width = input_weight.shape[2]
    groups = lax.axis_size("req")
    heads_axis = lax.axis_size("head")
    slot = width // heads_axis
    half = HD // 2
    frequencies = F32(ROPE_BASE) ** (-(2.0 / HD) * jnp.arange(half).astype(F32))
    down = shared_down.reshape(groups, shared_down.shape[0] // groups, shared_down.shape[1])
    down = lax.all_to_all(down, "req", split_axis=0, concat_axis=0, tiled=True)

    part, key, value, big, meta = attend(
        groups,
        heads_axis,
        frequencies[None],
        lengths,
        hidden_state,
        attend_gain[None],
        input_bias,
        sink_cache,
        expert_index.T,
        router_weight.T,
        jnp.transpose(input_weight, (1, 0, 2)),
        window_cache,
        output_weight,
    )
    new_kv = jnp.stack([key, value], axis=1)
    summed = part
    bit = 1
    while bit < heads_axis:
        summed = summed + lax.ppermute(
            summed, "head", [(j, j ^ bit) for j in range(heads_axis)]
        )
        bit *= 2

    summed, down = lax.optimization_barrier((summed, down))
    send, own = dispatch(
        groups, slot, summed, hidden_state, mixture_gain[None], shared_gate[None], big, meta
    )
    arrived = lax.all_to_all(send, "req", split_axis=0, concat_axis=0, tiled=True)
    sums = shared_in(groups, rows, arrived, shared_gate_up)
    sums = sums.reshape(groups, sums.shape[0] // groups, sums.shape[1])
    sums = lax.all_to_all(sums, "req", split_axis=0, concat_axis=0, tiled=True)
    routed = experts(groups, rows, arrived, expert_gate_up, expert_down)
    back = give_back(groups, heads_axis, rows, sums, down, routed, arrived)
    returned = lax.all_to_all(back, ("req", "head"), split_axis=0, concat_axis=0, tiled=True)
    return finish(returned, own), new_kv


def solution(mesh):
    return jax.shard_map(
        local,
        mesh=mesh,
        in_specs=(
            P("req", None),
            P(),
            P(None, None, "head"),
            P(None, "head"),
            P("head", None),
            P("req", None, None, "head"),
            P("req", None, None, "head"),
            P("req"),
            P("req", None),
            P("req", None),
            P(),
            P(None, ("req", "head"), None),
            P(("req", "head"), None),
            P(None, "req", "head"),
            P("head", "req"),
            P(),
        ),
        out_specs=(P("req", "head"), P("req", None, "head")),
        check_vma=False,
    )
```

time: 88.8 us -> 71.3 us (0.80)
  blocking collectives: 27.1 us -> 12.3 us
  local copies, waits for them, and re-layouts: 12.7 us -> 0.64 us
  starting transfers between devices: 12.8 us -> 17.7 us
  Pallas kernels: 21.3 us -> 24.9 us
  waiting for transfers between devices: 13.3 us -> 14.6 us
    all_to_all x1 -> x0, blocking collectives: 12 us -> none  [local(): sums = lax.all_to_all(sums, 'req', split_axis=0, concat_axis=0, tiled=True)]
    unnamed x23 -> x9, local copies, waits for them, and re-layouts: 11.9 us -> 0.64 us
    all_to_all x1 -> x2, starting transfers between devices: 3.39 us -> 10.7 us  [the longest x1 7.26 us: local(): down = lax.all_to_all(down, 'req', split_axis=0, concat_axis=0, tiled=True)]
    all_to_all x1, blocking collectives: 15.1 us -> 12.3 us  [local(): lax.all_to_all(send, 'req', split_axis=0, concat_axis=0, tiled=True)]
    pallas_call x1, Pallas kernels: 5.51 us -> 8.23 us  [experts(): pl.pallas_call(functools.partial(expert_kernel, groups, rows), out_shape=...]
    ppermute x2, starting transfers between devices: 3.45 us -> 1.66 us  [local(): lax.ppermute(summed, 'head', [(j, j ^ bit) for j in range(heads_axis)])]
    pallas_call x1, Pallas kernels: 12.3 us -> 13.5 us  [attend(): pl.pallas_call(functools.partial(attend_kernel, groups, heads_axis), out_...]
    pallas_call x2 -> x1, Pallas kernels: 1.58 us -> 0.65 us  [finish(): pl.pallas_call(finish_kernel, out_shape=jax.ShapeDtypeStruct(own.shape, B...]
  transfers between devices with their start and end apart: 4 -> 5, of which waited for: 3 -> 4; matrix products, arithmetic and copies ran while one was open for 1% -> 1% of each run, Pallas kernels for 6% -> 31%
where the time goes in v2:
time: 71.3 us; the launch traced here: 70.9 us
  Pallas kernels  24.9 us (35%)
  starting transfers between devices  17.7 us (25%)
  waiting for transfers between devices  14.6 us (20%)
  blocking collectives  12.3 us (17%)
  between operations  0.76 us (1%)
    pallas_call x1, Pallas kernels, attend(): pl.pallas_call(functools.partial(attend_kernel, groups, heads_axis), out_...  13.5 us
    all_to_all x1, blocking collectives, local(): lax.all_to_all(send, 'req', split_axis=0, concat_axis=0, tiled=True)  12.3 us
    all_to_all x1, waiting for transfers between devices, local(): lax.all_to_all(back, ('req', 'head'), split_axis=0, concat_axis=0, tiled=...  9.97 us
    pallas_call x1, Pallas kernels, experts(): pl.pallas_call(functools.partial(expert_kernel, groups, rows), out_shape=...  8.23 us
    all_to_all x1, starting transfers between devices, local(): down = lax.all_to_all(down, 'req', split_axis=0, concat_axis=0, tiled=True)  7.26 us
    all_to_all x1, starting transfers between devices, local(): lax.all_to_all(back, ('req', 'head'), split_axis=0, concat_axis=0, tiled=...  5.31 us
    ppermute x2, waiting for transfers between devices, local(): lax.ppermute(summed, 'head', [(j, j ^ bit) for j in range(heads_axis)])  3.99 us
    all_to_all x1, starting transfers between devices, local(): sums = lax.all_to_all(sums, 'req', split_axis=0, concat_axis=0, tiled=True)  3.44 us
  transfers between devices with their start and end apart: 5, of which 4 were waited for; matrix products, arithmetic and copies ran while one was open for 1% of the time, Pallas kernels for 31%

profile of v2, /device:TPU:0, one launch (start us, length us, event | category | flops | bytes accessed | tf_op | source)
XLA Modules:
  0.0 70.9 jit_solution(7997542584386955080)
XLA Ops:
  0.6 7.3 %all-to-all-start = ((bf16[8,176,256]{2,1,0:T(8,128)(2,1)}), bf16[8,176,256]{2,1,0:T(8,128)(2,1)S(1)}, u32[]{:S(2)}, u32[]{:S(2)}) async-start(bf16[8,176,256]{2,1,0:T(8,128)(2,1)} %bitcast.24), calls=%async_computation | async-start | bytes 1441792 | tf_op jit(solution)/shard_map/all_to_all | solution.py:566
  7.9 0.0 copy-start.1
  7.9 0.0 copy-start.2
  7.9 0.0 copy-start.3
  7.9 0.0 copy-start
  8.0 13.5 %attend.1 = (f32[8,2048]{1,0:T(8,128)S(1)}, bf16[8,512]{1,0:T(8,128)(2,1)S(1)}, bf16[8,512]{1,0:T(8,128)(2,1)S(1)}, bf16[192,64]{1,0:T(8,128)(2,1)S(1)}, bf16[64,256]{1,0:T(8,128)(2,1)S(1)}) custom-call(f32[1,64]{1,0:T(1,128)S(1)} %multiply_power_fusion.freq, s32[8]{0:T(128)} %lens_hbm.1, bf16[8,2048]{1,0:T(8,128)(2,1)} %hidden.1, f32[1,2048]{1,0:T(1,128)} %bitcast.25, ...), custom_call_target="tpu_custom_call" | custom-call | tf_op jit(solution)/shard_map/attend/pallas_call | solution.py:315
  21.5 0.1 collective-permute-start
  21.5 1.2 %collective-permute-done = f32[8,2048]{1,0:T(8,128)S(1)} collective-permute-done((f32[8,2048]{1,0:T(8,128)S(1)}, f32[8,2048]{1,0:T(8,128)S(1)}, u32[]{:S(2)}, u32[]{:S(2)}) %collective-permute-start) | collective-permute-done | bytes 65568 | tf_op jit(solution)/shard_map/ppermute | solution.py:587
  22.8 1.6 %collective-permute-start.1 = (f32[8,2048]{1,0:T(8,128)S(1)}, f32[8,2048]{1,0:T(8,128)S(1)}, u32[]{:S(2)}, u32[]{:S(2)}) collective-permute-start(f32[8,2048]{1,0:T(8,128)S(1)} %add.6), channel_id=1, source_target_pairs={{0,2},{1,3},{2,0},{3,1},{4,6},{5,7},{6,4},{7,5},{8,10},{9,11},{10,... | collective-permute-start | bytes 196616 | tf_op jit(solution)/shard_map/ppermute | solution.py:587
  24.4 2.7 %collective-permute-done.1 = f32[8,2048]{1,0:T(8,128)S(1)} collective-permute-done((f32[8,2048]{1,0:T(8,128)S(1)}, f32[8,2048]{1,0:T(8,128)S(1)}, u32[]{:S(2)}, u32[]{:S(2)}) %collective-permute-start.1) | collective-permute-done | bytes 65568 | tf_op jit(solution)/shard_map/ppermute | solution.py:587
  27.1 0.0 all-to-all-done.down
  27.1 0.0 copy-done.1
  27.2 0.0 copy-done.2
  27.2 0.0 copy-done.3
  27.2 0.3 dispatch.1
  27.4 12.3 %all_to_all.32 = bf16[8,32,256]{2,1,0:T(8,128)(2,1)S(1)} all-to-all(bf16[8,32,256]{2,1,0:T(8,128)(2,1)S(1)} %bitcast.18), channel_id=1, replica_groups=mesh['req'=8,'head'=4] {'req'}, dimensions={0} | all-to-all | bytes 262144 | tf_op jit(solution)/shard_map/all_to_all | solution.py:596
  39.7 0.0 copy-done
  39.8 1.2 %shared_in.1 = bf16[1408,128]{1,0:T(8,128)(2,1)} custom-call(bf16[256,256]{1,0:T(8,128)(2,1)S(1)} %bitcast.14, bf16[2,256,1408]{2,1,0:T(8,128)(2,1)S(1)} %copy-done), custom_call_target="tpu_custom_call" | custom-call | tf_op jit(solution)/shard_map/shared_in/pallas_call | solution.py:403
  40.9 3.4 %all-to-all-start.2 = ((bf16[8,176,128]{2,1,0:T(8,128)(2,1)}), bf16[8,176,128]{2,1,0:T(8,128)(2,1)S(1)}, u32[]{:S(2)}, u32[]{:S(2)}) async-start(bf16[8,176,128]{2,1,0:T(8,128)(2,1)} %bitcast.9), calls=%async_computation.2 | async-start | bytes 720896 | tf_op jit(solution)/shard_map/all_to_all | solution.py:599
  44.4 8.2 %experts.1.routed = f32[16,2048]{1,0:T(8,128)S(1)} custom-call(bf16[256,256]{1,0:T(8,128)(2,1)S(1)} %bitcast.15, bf16[2,1408,2048]{2,1,0:T(8,128)(2,1)} %gu_hbm.1, bf16[1408,2048]{1,0:T(8,128)(2,1)} %down_hbm.1), custom_call_target="tpu_custom_call" | custom-call | flops 276824064 | bytes 17301504 | tf_op jit(solution)/shard_map/experts/pallas_call | solution.py:457
  52.6 0.7 all-to-all-done.2.sums
  53.3 1.1 %give_back.1 = bf16[256,512]{1,0:T(8,128)(2,1)} custom-call(bf16[8,176,128]{2,1,0:T(8,128)(2,1)S(1)} %all-to-all-done.2.sums, bf16[8,176,256]{2,1,0:T(8,128)(2,1)S(1)} %all-to-all-done.down, f32[16,2048]{1,0:T(8,128)S(1)} %experts.1.routed, bf16[256,256]{1,0:T(8,128)(2,1)S(1)} %bitcast.16), custom_call_target="tpu_custom_call" | custom-call | tf_op jit(solution)/shard_map/give_back/pallas_call | solution.py:509
  54.4 5.3 %all-to-all-start.3 = ((bf16[32,8,512]{2,1,0:T(8,128)(2,1)}), bf16[32,8,512]{2,1,0:T(8,128)(2,1)S(1)}, u32[]{:S(2)}, u32[]{:S(2)}) async-start(bf16[32,8,512]{2,1,0:T(8,128)(2,1)} %bitcast.10), calls=%async_computation.3 | async-start | bytes 524288 | tf_op jit(solution)/shard_map/all_to_all | solution.py:602
  59.7 0.6 copy.18
  60.3 10.0 %all-to-all-done.3 = bf16[32,8,512]{2,1,0:T(8,128)(2,1)S(1)} async-done(((bf16[32,8,512]{2,1,0:T(8,128)(2,1)}), bf16[32,8,512]{2,1,0:T(8,128)(2,1)S(1)}, u32[]{:S(2)}, u32[]{:S(2)}) %all-to-all-start.3) | async-done | bytes 262176 | tf_op jit(solution)/shard_map/all_to_all | solution.py:602
  70.3 0.6 finish.1
  (4 shorter events, 0.0 us)
Async XLA Ops:
  0.6 26.5 %all-to-all-start = ((bf16[8,176,256]{2,1,0:T(8,128)(2,1)}), bf16[8,176,256]{2,1,0:T(8,128)(2,1)S(1)}, u32[]{:S(2)}, u32[]{:S(2)}) async-start(bf16[8,176,256]{2,1,0:T(8,128)(2,1)} %bitcast.24), calls=%async_computation | async-start | bytes 1441792 | tf_op jit(solution)/shard_map/all_to_all | solution.py:566
  7.9 19.2 %copy-start.1 = (bf16[8,2048]{1,0:T(8,128)(2,1)S(1)}, bf16[8,2048]{1,0:T(8,128)(2,1)}, u32[]{:S(2)}) copy-start(bf16[8,2048]{1,0:T(8,128)(2,1)} %hidden.1) | copy-start | bytes 98308
  7.9 19.2 %copy-start.2 = (f32[2048]{0:T(1024)S(1)}, f32[2048]{0:T(1024)}, u32[]{:S(2)}) copy-start(f32[2048]{0:T(1024)} %param.26) | copy-start | bytes 24580
  7.9 19.2 %copy-start.3 = (f32[2048]{0:T(1024)S(1)}, f32[2048]{0:T(1024)}, u32[]{:S(2)}) copy-start(f32[2048]{0:T(1024)} %param.31) | copy-start | bytes 24580
  7.9 31.8 %copy-start = (bf16[2,256,1408]{2,1,0:T(8,128)(2,1)S(1)}, bf16[2,256,1408]{2,1,0:T(8,128)(2,1)}, u32[]{:S(2)}) copy-start(bf16[2,256,1408]{2,1,0:T(8,128)(2,1)} %weights.1) | copy-start | bytes 4325380
  21.5 1.3 %collective-permute-start = (f32[8,2048]{1,0:T(8,128)S(1)}, f32[8,2048]{1,0:T(8,128)S(1)}, u32[]{:S(2)}, u32[]{:S(2)}) collective-permute-start(f32[8,2048]{1,0:T(8,128)S(1)} %get-tuple-element.11), channel_id=1, source_target_pairs={{0,1},{1,0},{2,3},{3,2},{4,5},{5,4},{6,7},{7,6},{8,9},{9,8},{10,11... | collective-permute-start | bytes 196616 | tf_op jit(solution)/shard_map/ppermute | solution.py:587
  22.8 4.3 %collective-permute-start.1 = (f32[8,2048]{1,0:T(8,128)S(1)}, f32[8,2048]{1,0:T(8,128)S(1)}, u32[]{:S(2)}, u32[]{:S(2)}) collective-permute-start(f32[8,2048]{1,0:T(8,128)S(1)} %add.6), channel_id=1, source_target_pairs={{0,2},{1,3},{2,0},{3,1},{4,6},{5,7},{6,4},{7,5},{8,10},{9,11},{10,... | collective-permute-start | bytes 196616 | tf_op jit(solution)/shard_map/ppermute | solution.py:587
  40.9 12.4 %all-to-all-start.2 = ((bf16[8,176,128]{2,1,0:T(8,128)(2,1)}), bf16[8,176,128]{2,1,0:T(8,128)(2,1)S(1)}, u32[]{:S(2)}, u32[]{:S(2)}) async-start(bf16[8,176,128]{2,1,0:T(8,128)(2,1)} %bitcast.9), calls=%async_computation.2 | async-start | bytes 720896 | tf_op jit(solution)/shard_map/all_to_all | solution.py:599
  54.4 15.9 %all-to-all-start.3 = ((bf16[32,8,512]{2,1,0:T(8,128)(2,1)}), bf16[32,8,512]{2,1,0:T(8,128)(2,1)S(1)}, u32[]{:S(2)}, u32[]{:S(2)}) async-start(bf16[32,8,512]{2,1,0:T(8,128)(2,1)} %bitcast.10), calls=%async_computation.3 | async-start | bytes 524288 | tf_op jit(solution)/shard_map/all_to_all | solution.py:602

commit v3 on v2

--- a/solution.py
+++ b/solution.py
@@ -18,6 +18,7 @@
 EPSILON = 1e-06
 ROPE_BASE = 1000000.0
 MB = 1 << 20
+SPAN = 384
 BF = jnp.bfloat16
 F32 = jnp.float32
 
@@ -119,8 +120,8 @@
     win_hbm,
     ow_hbm,
     part,
-    key_out,
-    value_out,
+    part_low,
+    new_kv,
     big_out,
     meta_out,
     lens,
@@ -235,8 +236,7 @@
     q = rotate(proj[0]).astype(BF).astype(F32)
     kf = rotate(proj[1]).astype(BF)
     vf = proj[2].astype(BF)
-    key_out[...] = kf
-    value_out[...] = vf
+    new_kv[...] = jnp.stack([kf.astype(F32), vf.astype(F32)], axis=1).astype(BF)
     head_mask = iota((ROWS, local), 1) // HD == iota((ROWS, local), 0)
     q3 = jnp.where(head_mask[None], q[:, None, :], 0.0)
     qbd[...] = q3.astype(BF)
@@ -303,7 +303,9 @@
     ]
     attended = jnp.concatenate(attended, axis=0).astype(BF)
     ow_copy.wait()
-    part[...] = dot(attended, ow_buf[...])
+    mine = dot(attended, ow_buf[...])
+    part[...] = mine
+    part_low[...] = mine.astype(BF)
 
 
 def attend(groups, heads_axis, freq, lens, hidden, gain, bias, sink, idx, rw, w, win, ow):
@@ -316,8 +318,8 @@
         functools.partial(attend_kernel, groups, heads_axis),
         out_shape=(
             jax.ShapeDtypeStruct((rows, width), F32),
-            jax.ShapeDtypeStruct((rows, local), BF),
-            jax.ShapeDtypeStruct((rows, local), BF),
+            jax.ShapeDtypeStruct((rows, width), BF),
+            jax.ShapeDtypeStruct((rows, 2, local), BF),
             jax.ShapeDtypeStruct((groups * span, groups * rows), BF),
             jax.ShapeDtypeStruct((groups * rows, width // groups), BF),
         ),
@@ -348,9 +350,13 @@
     )(freq, *map(stay, (lens, hidden, gain, bias, sink, idx, rw, w, win, ow)))
 
 
-def dispatch_kernel(groups, summed, hidden, gain, gate_vec, big, meta, send, own_out, keep):
+def dispatch_kernel(groups, others, mine, hidden, gain, gate_vec, big, meta, *rest):
+    parts, (send, own_out, keep) = rest[:others], rest[others:]
     rows, width = hidden.shape
-    resid = hidden[...].astype(F32) + summed[...]
+    summed = mine[...]
+    for p in parts:
+        summed = summed + p[...].astype(F32)
+    resid = hidden[...].astype(F32) + summed
     keep[...] = resid
     ms = jnp.mean(resid * resid, axis=-1, keepdims=True)
     tokens = (resid * lax.rsqrt(ms + EPSILON) * gain[...]).astype(BF).astype(F32)
@@ -373,38 +379,50 @@
     own_out[...] = keep[:, pl.ds(start, slot)]
 
 
-def dispatch(groups, slot, summed, hidden, gain, gate_vec, big, meta):
+def dispatch(groups, slot, mine, parts, hidden, gain, gate_vec, big, meta):
     rows, width = hidden.shape
     return pl.pallas_call(
-        functools.partial(dispatch_kernel, groups),
+        functools.partial(dispatch_kernel, groups, len(parts)),
         out_shape=(
             jax.ShapeDtypeStruct((big.shape[0] + groups * rows, width // groups), BF),
             jax.ShapeDtypeStruct((rows, slot), F32),
         ),
-        in_specs=[VM] * 6,
+        in_specs=[VM] * (6 + len(parts)),
         out_specs=(VM,) * 2,
         scratch_shapes=[pltpu.VMEM((rows, width), F32)],
         compiler_params=params(16 * MB),
         name="dispatch",
-    )(summed, hidden, gain, gate_vec, big, meta)
-
-
-def shared_in_kernel(groups, rows, arrived, weights, out):
+    )(mine, hidden, gain, gate_vec, big, meta, *parts)
+
+
+def shared_in_kernel(groups, rows, arrived, weights, out, buf, sem):
     span = arrived.shape[0] // groups
     x = jnp.concatenate(
         [arrived[g * span : g * span + rows, :] for g in range(groups)], axis=0
     )
     tokens = x.shape[0]
-    both = jnp.concatenate([dot(x, weights[0]), dot(x, weights[1])], axis=0)
-    out[...] = both.T.astype(BF)
+    copies = []
+    for i, first in enumerate(range(0, weights.shape[2], SPAN)):
+        at = slice(first, min(first + SPAN, weights.shape[2]))
+        both = jnp.concatenate([dot(x, weights[0, :, at]), dot(x, weights[1, :, at])], axis=0)
+        buf[at, :] = both.T.astype(BF)
+        copies.append(pltpu.make_async_copy(buf.at[at], out.at[at], sem.at[i]))
+        copies[-1].start()
+    for copy in copies:
+        copy.wait()
 
 
 def shared_in(groups, rows, arrived, weights):
+    shape = (weights.shape[2], 2 * groups * rows)
     return pl.pallas_call(
         functools.partial(shared_in_kernel, groups, rows),
-        out_shape=jax.ShapeDtypeStruct((weights.shape[2], 2 * groups * rows), BF),
+        out_shape=jax.ShapeDtypeStruct(shape, BF),
         in_specs=[VM] * 2,
-        out_specs=VM,
+        out_specs=HB,
+        scratch_shapes=[
+            pltpu.VMEM(shape, BF),
+            pltpu.SemaphoreType.DMA((pl.cdiv(shape[0], SPAN),)),
+        ],
         compiler_params=params(16 * MB),
         name="shared_in",
     )(arrived, weights)
@@ -425,6 +443,7 @@
     for i in range(pieces):
         gu_copy(0, i).start()
         gu_copy(1, i).start()
+    for i in range(pieces):
         down_copy(i).start()
 
     slots = groups * CAP
@@ -437,16 +456,18 @@
     x = jnp.concatenate(
         [x[jj * slots : (jj + 1) * slots, :] for jj in range(groups)], axis=1
     ).astype(BF)
-    result = jnp.zeros((slots, down.shape[1]), F32)
+    hidden = []
     for i in range(pieces):
         at = slice(i * piece, (i + 1) * piece)
         gu_copy(0, i).wait()
         gate = lax.dot_general(x, gu[0, at, :], NT, preferred_element_type=F32)
         gu_copy(1, i).wait()
         up = lax.dot_general(x, gu[1, at, :], NT, preferred_element_type=F32)
-        hidden = (jax.nn.silu(gate) * up).astype(BF)
+        hidden.append((jax.nn.silu(gate) * up).astype(BF))
+    result = jnp.zeros((slots, down.shape[1]), F32)
+    for i in range(pieces):
         down_copy(i).wait()
-        result = result + dot(hidden, down[at, :])
+        result = result + dot(hidden[i], down[i * piece : (i + 1) * piece, :])
     out[...] = result
 
 
@@ -565,7 +586,7 @@
     down = shared_down.reshape(groups, shared_down.shape[0] // groups, shared_down.shape[1])
     down = lax.all_to_all(down, "req", split_axis=0, concat_axis=0, tiled=True)
 
-    part, key, value, big, meta = attend(
+    part, low, new_kv, big, meta = attend(
         groups,
         heads_axis,
         frequencies[None],
@@ -580,18 +601,13 @@
         window_cache,
         output_weight,
     )
-    new_kv = jnp.stack([key, value], axis=1)
-    summed = part
-    bit = 1
-    while bit < heads_axis:
-        summed = summed + lax.ppermute(
-            summed, "head", [(j, j ^ bit) for j in range(heads_axis)]
-        )
-        bit *= 2
-
-    summed, down = lax.optimization_barrier((summed, down))
+    parts = [
+        lax.ppermute(part if k == 1 else low, "head", [(j, j ^ k) for j in range(heads_axis)])
+        for k in range(1, heads_axis)
+    ]
+    parts, down = lax.optimization_barrier((parts, down))
     send, own = dispatch(
-        groups, slot, summed, hidden_state, mixture_gain[None], shared_gate[None], big, meta
+        groups, slot, part, parts, hidden_state, mixture_gain[None], shared_gate[None], big, meta
     )
     arrived = lax.all_to_all(send, "req", split_axis=0, concat_axis=0, tiled=True)
     sums = shared_in(groups, rows, arrived, shared_gate_up)

time: 71.3 us -> 69.6 us (0.976)
  blocking collectives: 12.3 us -> 26.5 us
  waiting for transfers between devices: 14.6 us -> 5.07 us
  starting transfers between devices: 17.7 us -> 12.7 us
    all_to_all x0 -> x1, blocking collectives: none -> 13.9 us  [local(): lax.all_to_all(back, ('req', 'head'), split_axis=0, concat_axis=0, tiled=...]
    all_to_all x1 -> x0, waiting for transfers between devices: 9.97 us -> none  [local(): lax.all_to_all(back, ('req', 'head'), split_axis=0, concat_axis=0, tiled=...]
    all_to_all x1 -> x0, starting transfers between devices: 5.31 us -> none  [local(): lax.all_to_all(back, ('req', 'head'), split_axis=0, concat_axis=0, tiled=...]
    all_to_all x1, waiting for transfers between devices: 0.68 us -> 1.86 us  [local(): sums = lax.all_to_all(sums, 'req', split_axis=0, concat_axis=0, tiled=True)]
    ppermute x2 -> x3, waiting for transfers between devices: 3.99 us -> 3.07 us  [local(): lax.ppermute(part if k == 1 else low, 'head', [(j, j ^ k) for j in range(...]
    ppermute x2 -> x3, starting transfers between devices: 1.66 us -> 1.93 us  [local(): lax.ppermute(part if k == 1 else low, 'head', [(j, j ^ k) for j in range(...]
  transfers between devices with their start and end apart: 5 -> 5, of which waited for: 4 -> 4; matrix products, arithmetic and copies ran while one was open for 1% -> 0% of each run, Pallas kernels for 31% -> 31%
where the time goes in v3:
time: 69.6 us; the launch traced here: 69.1 us
  blocking collectives  26.5 us (38%)
  Pallas kernels  24.2 us (35%)
  starting transfers between devices  12.7 us (18%)
  waiting for transfers between devices  5.07 us (7%)
  between operations  0.72 us (1%)
    all_to_all x1, blocking collectives, local(): lax.all_to_all(back, ('req', 'head'), split_axis=0, concat_axis=0, tiled=...  13.9 us
    pallas_call x1, Pallas kernels, attend(): pl.pallas_call(functools.partial(attend_kernel, groups, heads_axis), out_...  13.5 us
    all_to_all x1, blocking collectives, local(): lax.all_to_all(send, 'req', split_axis=0, concat_axis=0, tiled=True)  12.6 us
    pallas_call x1, Pallas kernels, experts(): pl.pallas_call(functools.partial(expert_kernel, groups, rows), out_shape=...  8.23 us
    all_to_all x1, starting transfers between devices, local(): down = lax.all_to_all(down, 'req', split_axis=0, concat_axis=0, tiled=True)  7.26 us
    all_to_all x1, starting transfers between devices, local(): sums = lax.all_to_all(sums, 'req', split_axis=0, concat_axis=0, tiled=True)  3.45 us
    ppermute x3, waiting for transfers between devices, local(): lax.ppermute(part if k == 1 else low, 'head', [(j, j ^ k) for j in range(...  3.07 us
    ppermute x3, starting transfers between devices, local(): lax.ppermute(part if k == 1 else low, 'head', [(j, j ^ k) for j in range(...  1.93 us
  transfers between devices with their start and end apart: 5, of which 4 were waited for; matrix products, arithmetic and copies ran while one was open for 0% of the time, Pallas kernels for 31%

profile of v3, /device:TPU:0, one launch (start us, length us, event | category | flops | bytes accessed | tf_op | source)
XLA Modules:
  0.0 69.1 jit_solution(10583583350479055764)
XLA Ops:
  0.6 7.3 %all-to-all-start = ((bf16[8,176,256]{2,1,0:T(8,128)(2,1)}), bf16[8,176,256]{2,1,0:T(8,128)(2,1)S(1)}, u32[]{:S(2)}, u32[]{:S(2)}) async-start(bf16[8,176,256]{2,1,0:T(8,128)(2,1)} %bitcast.21), calls=%async_computation | async-start | bytes 1441792 | tf_op jit(solution)/shard_map/all_to_all | solution.py:587
  7.9 0.0 copy-start.1
  7.9 0.0 copy-start.2
  7.9 0.0 copy-start.3
  7.9 0.0 copy-start
  8.0 13.5 %attend.1 = (f32[8,2048]{1,0:T(8,128)S(1)}, bf16[8,2048]{1,0:T(8,128)(2,1)S(1)}, bf16[8,2,512]{2,1,0:T(2,128)(2,1)}, bf16[192,64]{1,0:T(8,128)(2,1)S(1)}, bf16[64,256]{1,0:T(8,128)(2,1)S(1)}) custom-call(f32[1,64]{1,0:T(1,128)S(1)} %multiply_power_fusion.freq, s32[8]{0:T(128)} %lens_hbm.1, bf16[8,2048]{1,0:T(8,128)(2,1)} %hidden.1, f32[1,2048]{1,0:T(1,128)} %bitcast.22, ...), custom_call_target="tpu_custom_call" | custom-call | tf_op jit(solution)/shard_map/attend/pallas_call | solution.py:317
  21.5 0.1 collective-permute-start
  21.5 1.6 %collective-permute-start.1 = (bf16[8,2048]{1,0:T(8,128)(2,1)S(1)}, bf16[8,2048]{1,0:T(8,128)(2,1)S(1)}, u32[]{:S(2)}, u32[]{:S(2)}) collective-permute-start(bf16[8,2048]{1,0:T(8,128)(2,1)S(1)} %get-tuple-element.16), channel_id=1, source_target_pairs={{0,2},{1,3},{2,0},{3,1},{4,6},{5,7},{6,4},{7,5},{8,10},{9,11},{10,... | collective-permute-start | bytes 98312 | tf_op jit(solution)/shard_map/ppermute | solution.py:605
  23.1 0.3 collective-permute-start.2
  23.4 2.1 %collective-permute-done.1.rest_1_ = bf16[8,2048]{1,0:T(8,128)(2,1)S(1)} collective-permute-done((bf16[8,2048]{1,0:T(8,128)(2,1)S(1)}, bf16[8,2048]{1,0:T(8,128)(2,1)S(1)}, u32[]{:S(2)}, u32[]{:S(2)}) %collective-permute-start.1) | collective-permute-done | bytes 32800 | tf_op jit(solution)/shard_map/ppermute | solution.py:605
  25.5 1.0 %collective-permute-done.2.rest_2_ = bf16[8,2048]{1,0:T(8,128)(2,1)S(1)} collective-permute-done((bf16[8,2048]{1,0:T(8,128)(2,1)S(1)}, bf16[8,2048]{1,0:T(8,128)(2,1)S(1)}, u32[]{:S(2)}, u32[]{:S(2)}) %collective-permute-start.2) | collective-permute-done | bytes 32800 | tf_op jit(solution)/shard_map/ppermute | solution.py:605
  26.5 0.0 collective-permute-done.rest_0_
  26.5 0.1 all-to-all-done.down
  26.6 0.0 copy-done.1
  26.6 0.0 copy-done.2
  26.6 0.0 copy-done.3
  26.6 0.3 dispatch.1
  26.9 12.6 %all_to_all.32 = bf16[8,32,256]{2,1,0:T(8,128)(2,1)S(1)} all-to-all(bf16[8,32,256]{2,1,0:T(8,128)(2,1)S(1)} %bitcast.17), channel_id=1, replica_groups=mesh['req'=8,'head'=4] {'req'}, dimensions={0} | all-to-all | bytes 262144 | tf_op jit(solution)/shard_map/all_to_all | solution.py:612
  39.5 0.0 copy-done
  39.5 1.1 %shared_in.1 = bf16[1408,128]{1,0:T(8,128)(2,1)} custom-call(bf16[256,256]{1,0:T(8,128)(2,1)S(1)} %bitcast.12, bf16[2,256,1408]{2,1,0:T(8,128)(2,1)S(1)} %copy-done), custom_call_target="tpu_custom_call" | custom-call | tf_op jit(solution)/shard_map/shared_in/pallas_call | solution.py:417
  40.6 3.5 %all-to-all-start.2 = ((bf16[8,176,128]{2,1,0:T(8,128)(2,1)}), bf16[8,176,128]{2,1,0:T(8,128)(2,1)S(1)}, u32[]{:S(2)}, u32[]{:S(2)}) async-start(bf16[8,176,128]{2,1,0:T(8,128)(2,1)} %bitcast.9), calls=%async_computation.2 | async-start | bytes 720896 | tf_op jit(solution)/shard_map/all_to_all | solution.py:615
  44.1 8.2 %experts.1.routed = f32[16,2048]{1,0:T(8,128)S(1)} custom-call(bf16[256,256]{1,0:T(8,128)(2,1)S(1)} %bitcast.13, bf16[2,1408,2048]{2,1,0:T(8,128)(2,1)} %gu_hbm.1, bf16[1408,2048]{1,0:T(8,128)(2,1)} %down_hbm.1), custom_call_target="tpu_custom_call" | custom-call | flops 276824064 | bytes 17301504 | tf_op jit(solution)/shard_map/experts/pallas_call | solution.py:478
  52.3 1.9 %all-to-all-done.2.sums = bf16[8,176,128]{2,1,0:T(8,128)(2,1)S(1)} async-done(((bf16[8,176,128]{2,1,0:T(8,128)(2,1)}), bf16[8,176,128]{2,1,0:T(8,128)(2,1)S(1)}, u32[]{:S(2)}, u32[]{:S(2)}) %all-to-all-start.2) | async-done | bytes 360480 | tf_op jit(solution)/shard_map/all_to_all | solution.py:615
  54.2 0.4 give_back.1
  54.6 13.9 %all_to_all.33 = bf16[32,8,512]{2,1,0:T(8,128)(2,1)S(1)} all-to-all(bf16[32,8,512]{2,1,0:T(8,128)(2,1)S(1)} %bitcast.15), channel_id=1, replica_groups=mesh['req'=8,'head'=4] {'req','head'}, dimensions={0} | all-to-all | bytes 524288 | tf_op jit(solution)/shard_map/all_to_all | solution.py:618
  68.5 0.6 finish.1
  (1 shorter events, 0.0 us)
Async XLA Ops:
  0.6 26.0 %all-to-all-start = ((bf16[8,176,256]{2,1,0:T(8,128)(2,1)}), bf16[8,176,256]{2,1,0:T(8,128)(2,1)S(1)}, u32[]{:S(2)}, u32[]{:S(2)}) async-start(bf16[8,176,256]{2,1,0:T(8,128)(2,1)} %bitcast.21), calls=%async_computation | async-start | bytes 1441792 | tf_op jit(solution)/shard_map/all_to_all | solution.py:587
  7.9 18.7 %copy-start.1 = (bf16[8,2048]{1,0:T(8,128)(2,1)S(1)}, bf16[8,2048]{1,0:T(8,128)(2,1)}, u32[]{:S(2)}) copy-start(bf16[8,2048]{1,0:T(8,128)(2,1)} %hidden.1) | copy-start | bytes 98308
  7.9 18.7 %copy-start.2 = (f32[2048]{0:T(1024)S(1)}, f32[2048]{0:T(1024)}, u32[]{:S(2)}) copy-start(f32[2048]{0:T(1024)} %param.26) | copy-start | bytes 24580
  7.9 18.7 %copy-start.3 = (f32[2048]{0:T(1024)S(1)}, f32[2048]{0:T(1024)}, u32[]{:S(2)}) copy-start(f32[2048]{0:T(1024)} %param.31) | copy-start | bytes 24580
  7.9 31.6 %copy-start = (bf16[2,256,1408]{2,1,0:T(8,128)(2,1)S(1)}, bf16[2,256,1408]{2,1,0:T(8,128)(2,1)}, u32[]{:S(2)}) copy-start(bf16[2,256,1408]{2,1,0:T(8,128)(2,1)} %weights.1) | copy-start | bytes 4325380
  21.5 5.0 %collective-permute-start = (f32[8,2048]{1,0:T(8,128)S(1)}, f32[8,2048]{1,0:T(8,128)S(1)}, u32[]{:S(2)}, u32[]{:S(2)}) collective-permute-start(f32[8,2048]{1,0:T(8,128)S(1)} %get-tuple-element.13.mine), channel_id=1, source_target_pairs={{0,1},{1,0},{2,3},{3,2},{4,5},{5,4},{6,7},{7,6},{8,9},{9,8},{10,11... | collective-permute-start | bytes 196616 | tf_op jit(solution)/shard_map/ppermute | solution.py:605
  21.5 4.0 %collective-permute-start.1 = (bf16[8,2048]{1,0:T(8,128)(2,1)S(1)}, bf16[8,2048]{1,0:T(8,128)(2,1)S(1)}, u32[]{:S(2)}, u32[]{:S(2)}) collective-permute-start(bf16[8,2048]{1,0:T(8,128)(2,1)S(1)} %get-tuple-element.16), channel_id=1, source_target_pairs={{0,2},{1,3},{2,0},{3,1},{4,6},{5,7},{6,4},{7,5},{8,10},{9,11},{10,... | collective-permute-start | bytes 98312 | tf_op jit(solution)/shard_map/ppermute | solution.py:605
  23.1 3.3 %collective-permute-start.2 = (bf16[8,2048]{1,0:T(8,128)(2,1)S(1)}, bf16[8,2048]{1,0:T(8,128)(2,1)S(1)}, u32[]{:S(2)}, u32[]{:S(2)}) collective-permute-start(bf16[8,2048]{1,0:T(8,128)(2,1)S(1)} %get-tuple-element.16), channel_id=1, source_target_pairs={{0,3},{1,2},{2,1},{3,0},{4,7},{5,6},{6,5},{7,4},{8,11},{9,10},{10,... | collective-permute-start | bytes 98312 | tf_op jit(solution)/shard_map/ppermute | solution.py:605
  40.6 13.6 %all-to-all-start.2 = ((bf16[8,176,128]{2,1,0:T(8,128)(2,1)}), bf16[8,176,128]{2,1,0:T(8,128)(2,1)S(1)}, u32[]{:S(2)}, u32[]{:S(2)}) async-start(bf16[8,176,128]{2,1,0:T(8,128)(2,1)} %bitcast.9), calls=%async_computation.2 | async-start | bytes 720896 | tf_op jit(solution)/shard_map/all_to_all | solution.py:615

commit v4 on v3

--- a/solution.py
+++ b/solution.py
@@ -18,7 +18,6 @@
 EPSILON = 1e-06
 ROPE_BASE = 1000000.0
 MB = 1 << 20
-SPAN = 384
 BF = jnp.bfloat16
 F32 = jnp.float32
 
@@ -321,7 +320,7 @@
             jax.ShapeDtypeStruct((rows, width), BF),
             jax.ShapeDtypeStruct((rows, 2, local), BF),
             jax.ShapeDtypeStruct((groups * span, groups * rows), BF),
-            jax.ShapeDtypeStruct((groups * rows, width // groups), BF),
+            jax.ShapeDtypeStruct((groups * rows, 2 * groups * rows), BF),
         ),
         in_specs=[VM] + [HB] * 10,
         out_specs=(VM,) * 5,
@@ -351,7 +350,7 @@
 
 
 def dispatch_kernel(groups, others, mine, hidden, gain, gate_vec, big, meta, *rest):
-    parts, (send, own_out, keep) = rest[:others], rest[others:]
+    parts, (send, meta_out, own_out, keep) = rest[:others], rest[others:]
     rows, width = hidden.shape
     summed = mine[...]
     for p in parts:
@@ -364,16 +363,14 @@
     w = width // groups
     stacked = jnp.concatenate([tokens[:, j * w : (j + 1) * w] for j in range(groups)], axis=0)
     placed = dot(big[...], stacked.astype(BF)).astype(BF)
-    lane = iota((rows, w), 1)
-    extra = jnp.zeros((rows, w), F32)
+    lane = iota((rows, meta.shape[1]), 1)
+    extra = jnp.zeros((rows, meta.shape[1]), F32)
     for p, term in enumerate(split3(gate)):
         extra = extra + jnp.where(lane == 3 * CAP + p, term, 0.0)
-    span = placed.shape[0] // groups
-    full = send.shape[0] // groups
+    send[...] = placed
     for g in range(groups):
-        send[g * full : g * full + span, :] = placed[g * span : (g + 1) * span, :]
-        told = meta[g * rows : (g + 1) * rows, :].astype(F32) + extra
-        send[g * full + span : (g + 1) * full, :] = told.astype(BF)
+        at = slice(g * rows, (g + 1) * rows)
+        meta_out[at, :] = (meta[at, :].astype(F32) + extra).astype(BF)
     slot = own_out.shape[1]
     start = pl.multiple_of(lax.axis_index("head") * slot, HD)
     own_out[...] = keep[:, pl.ds(start, slot)]
@@ -384,48 +381,40 @@
     return pl.pallas_call(
         functools.partial(dispatch_kernel, groups, len(parts)),
         out_shape=(
-            jax.ShapeDtypeStruct((big.shape[0] + groups * rows, width // groups), BF),
+            jax.ShapeDtypeStruct((big.shape[0], width // groups), BF),
+            jax.ShapeDtypeStruct(meta.shape, BF),
             jax.ShapeDtypeStruct((rows, slot), F32),
         ),
         in_specs=[VM] * (6 + len(parts)),
-        out_specs=(VM,) * 2,
+        out_specs=(VM,) * 3,
         scratch_shapes=[pltpu.VMEM((rows, width), F32)],
         compiler_params=params(16 * MB),
         name="dispatch",
     )(mine, hidden, gain, gate_vec, big, meta, *parts)
 
 
-def shared_in_kernel(groups, rows, arrived, weights, out, buf, sem):
+def shared_in_kernel(groups, rows, arrived, weights, meta, out):
     span = arrived.shape[0] // groups
     x = jnp.concatenate(
         [arrived[g * span : g * span + rows, :] for g in range(groups)], axis=0
     )
-    tokens = x.shape[0]
-    copies = []
-    for i, first in enumerate(range(0, weights.shape[2], SPAN)):
-        at = slice(first, min(first + SPAN, weights.shape[2]))
-        both = jnp.concatenate([dot(x, weights[0, :, at]), dot(x, weights[1, :, at])], axis=0)
-        buf[at, :] = both.T.astype(BF)
-        copies.append(pltpu.make_async_copy(buf.at[at], out.at[at], sem.at[i]))
-        copies[-1].start()
-    for copy in copies:
-        copy.wait()
-
-
-def shared_in(groups, rows, arrived, weights):
-    shape = (weights.shape[2], 2 * groups * rows)
+    both = jnp.concatenate([dot(x, weights[0]), dot(x, weights[1])], axis=0).T
+    piece = both.shape[0] // groups
+    for g in range(groups):
+        out[g, :piece, :] = both[g * piece : (g + 1) * piece, :].astype(BF)
+        out[g, piece:, :] = meta[g * rows : (g + 1) * rows, :]
+
+
+def shared_in(groups, rows, arrived, weights, meta):
+    piece = weights.shape[2] // groups
     return pl.pallas_call(
         functools.partial(shared_in_kernel, groups, rows),
-        out_shape=jax.ShapeDtypeStruct(shape, BF),
-        in_specs=[VM] * 2,
-        out_specs=HB,
-        scratch_shapes=[
-            pltpu.VMEM(shape, BF),
-            pltpu.SemaphoreType.DMA((pl.cdiv(shape[0], SPAN),)),
-        ],
+        out_shape=jax.ShapeDtypeStruct((groups, piece + rows, 2 * groups * rows), BF),
+        in_specs=[VM] * 3,
+        out_specs=VM,
         compiler_params=params(16 * MB),
         name="shared_in",
-    )(arrived, weights)
+    )(arrived, weights, meta)
 
 
 def expert_kernel(groups, rows, arrived, gu_hbm, down_hbm, out, gu, down, gu_sem, down_sem):
@@ -494,17 +483,17 @@
     )(arrived, stay(gate_up), stay(down))
 
 
-def give_back_kernel(groups, heads_axis, rows, sums, down, routed, arrived, out):
-    total = sums[0].astype(F32)
+def give_back_kernel(groups, heads_axis, rows, sums, down, routed, out):
+    piece = down.shape[1]
+    total = sums[0, :piece, :].astype(F32)
     for g in range(1, groups):
-        total = total + sums[g].astype(F32)
+        total = total + sums[g, :piece, :].astype(F32)
     tokens = groups * rows
     hidden = jax.nn.silu(total) * pltpu.roll(total, tokens, 1)
     hidden = hidden[:, :tokens].T.astype(BF)
-    span = arrived.shape[0] // groups
     told = jnp.concatenate(
-        [arrived[(g + 1) * span - rows : (g + 1) * span, :HD] for g in range(groups)], axis=0
-    ).astype(F32)
+        [sums[g, piece:, :].astype(F32)[:, :HD] for g in range(groups)], axis=0
+    )
 
     def column(k):
         return told[:, 3 * k : 3 * k + 1] + told[:, 3 * k + 1 : 3 * k + 2] + told[:, 3 * k + 2 : 3 * k + 3]
@@ -526,17 +515,17 @@
             out[to : to + rows, half * w : (half + 1) * w] = value.astype(BF)
 
 
-def give_back(groups, heads_axis, rows, sums, down, routed, arrived):
+def give_back(groups, heads_axis, rows, sums, down, routed):
     return pl.pallas_call(
         functools.partial(give_back_kernel, groups, heads_axis, rows),
         out_shape=jax.ShapeDtypeStruct(
             (groups * heads_axis * rows, routed.shape[1] // heads_axis), BF
         ),
-        in_specs=[VM] * 4,
+        in_specs=[VM] * 3,
         out_specs=VM,
         compiler_params=params(16 * MB),
         name="give_back",
-    )(sums, down, routed, arrived)
+    )(sums, down, routed)
 
 
 def finish_kernel(returned, own, out):
@@ -606,15 +595,14 @@
         for k in range(1, heads_axis)
     ]
     parts, down = lax.optimization_barrier((parts, down))
-    send, own = dispatch(
+    send, meta, own = dispatch(
         groups, slot, part, parts, hidden_state, mixture_gain[None], shared_gate[None], big, meta
     )
     arrived = lax.all_to_all(send, "req", split_axis=0, concat_axis=0, tiled=True)
-    sums = shared_in(groups, rows, arrived, shared_gate_up)
-    sums = sums.reshape(groups, sums.shape[0] // groups, sums.shape[1])
+    sums = shared_in(groups, rows, arrived, shared_gate_up, meta)
     sums = lax.all_to_all(sums, "req", split_axis=0, concat_axis=0, tiled=True)
     routed = experts(groups, rows, arrived, expert_gate_up, expert_down)
-    back = give_back(groups, heads_axis, rows, sums, down, routed, arrived)
+    back = give_back(groups, heads_axis, rows, sums, down, routed)
     returned = lax.all_to_all(back, ("req", "head"), split_axis=0, concat_axis=0, tiled=True)
     return finish(returned, own), new_kv
 

time: 69.6 us -> 70.2 us (level)
  Pallas kernels: 24.2 us -> 25 us
    pallas_call x1, Pallas kernels: 13.5 us -> 14.3 us  [attend(): pl.pallas_call(functools.partial(attend_kernel, groups, heads_axis), out_...]
  transfers between devices with their start and end apart: 5 -> 5, of which waited for: 4 -> 3; matrix products, arithmetic and copies ran while one was open for 0% -> 0% of each run, Pallas kernels for 31% -> 32%
where the time goes in v4:
time: 70.2 us
  blocking collectives  26.4 us (38%)
  Pallas kernels  25 us (36%)
  starting transfers between devices  12.6 us (18%)
  waiting for transfers between devices  5.32 us (8%)
  between operations  0.73 us (1%)
    pallas_call x1, Pallas kernels, attend(): pl.pallas_call(functools.partial(attend_kernel, groups, heads_axis), out_...  14.3 us
    all_to_all x1, blocking collectives, local(): lax.all_to_all(back, ('req', 'head'), split_axis=0, concat_axis=0, tiled=...  13.5 us
    all_to_all x1, blocking collectives, local(): lax.all_to_all(send, 'req', split_axis=0, concat_axis=0, tiled=True)  12.9 us
    pallas_call x1, Pallas kernels, experts(): pl.pallas_call(functools.partial(expert_kernel, groups, rows), out_shape=...  8.18 us
    all_to_all x1, starting transfers between devices, local(): down = lax.all_to_all(down, 'req', split_axis=0, concat_axis=0, tiled=True)  7.26 us
    all_to_all x1, starting transfers between devices, local(): sums = lax.all_to_all(sums, 'req', split_axis=0, concat_axis=0, tiled=True)  3.45 us
    ppermute x3, waiting for transfers between devices, local(): lax.ppermute(part if k == 1 else low, 'head', [(j, j ^ k) for j in range(...  3.07 us
    all_to_all x1, waiting for transfers between devices, local(): sums = lax.all_to_all(sums, 'req', split_axis=0, concat_axis=0, tiled=True)  2.25 us
  transfers between devices with their start and end apart: 5, of which 3 were waited for; matrix products, arithmetic and copies ran while one was open for 0% of the time, Pallas kernels for 32%

profile of v4, /device:TPU:0, one launch (start us, length us, event | category | flops | bytes accessed | tf_op | source)
XLA Modules:
  0.0 70.2 jit_solution(9120685188112466730)
XLA Ops:
  0.6 7.3 %all-to-all-start = ((bf16[8,176,256]{2,1,0:T(8,128)(2,1)}), bf16[8,176,256]{2,1,0:T(8,128)(2,1)S(1)}, u32[]{:S(2)}, u32[]{:S(2)}) async-start(bf16[8,176,256]{2,1,0:T(8,128)(2,1)} %bitcast.19), calls=%async_computation | async-start | bytes 1441792 | tf_op jit(solution)/shard_map/all_to_all | solution.py:576
  7.9 0.0 copy-start.1
  7.9 0.0 copy-start.2
  7.9 0.0 copy-start.3
  7.9 0.0 copy-start
  8.0 14.3 %attend.1 = (f32[8,2048]{1,0:T(8,128)S(1)}, bf16[8,2048]{1,0:T(8,128)(2,1)S(1)}, bf16[8,2,512]{2,1,0:T(2,128)(2,1)}, bf16[192,64]{1,0:T(8,128)(2,1)S(1)}, bf16[64,128]{1,0:T(8,128)(2,1)S(1)}) custom-call(f32[1,64]{1,0:T(1,128)S(1)} %multiply_power_fusion.freq, s32[8]{0:T(128)} %lens_hbm.1, bf16[8,2048]{1,0:T(8,128)(2,1)} %hidden.1, f32[1,2048]{1,0:T(1,128)} %bitcast.20, ...), custom_call_target="tpu_custom_call" | custom-call | tf_op jit(solution)/shard_map/attend/pallas_call | solution.py:316
  22.3 0.1 collective-permute-start
  22.4 1.6 %collective-permute-start.1 = (bf16[8,2048]{1,0:T(8,128)(2,1)S(1)}, bf16[8,2048]{1,0:T(8,128)(2,1)S(1)}, u32[]{:S(2)}, u32[]{:S(2)}) collective-permute-start(bf16[8,2048]{1,0:T(8,128)(2,1)S(1)} %get-tuple-element.17), channel_id=1, source_target_pairs={{0,2},{1,3},{2,0},{3,1},{4,6},{5,7},{6,4},{7,5},{8,10},{9,11},{10,... | collective-permute-start | bytes 98312 | tf_op jit(solution)/shard_map/ppermute | solution.py:594
  24.0 0.3 collective-permute-start.2
  24.2 2.1 %collective-permute-done.1.rest_1_ = bf16[8,2048]{1,0:T(8,128)(2,1)S(1)} collective-permute-done((bf16[8,2048]{1,0:T(8,128)(2,1)S(1)}, bf16[8,2048]{1,0:T(8,128)(2,1)S(1)}, u32[]{:S(2)}, u32[]{:S(2)}) %collective-permute-start.1) | collective-permute-done | bytes 32800 | tf_op jit(solution)/shard_map/ppermute | solution.py:594
  26.4 1.0 %collective-permute-done.2.rest_2_ = bf16[8,2048]{1,0:T(8,128)(2,1)S(1)} collective-permute-done((bf16[8,2048]{1,0:T(8,128)(2,1)S(1)}, bf16[8,2048]{1,0:T(8,128)(2,1)S(1)}, u32[]{:S(2)}, u32[]{:S(2)}) %collective-permute-start.2) | collective-permute-done | bytes 32800 | tf_op jit(solution)/shard_map/ppermute | solution.py:594
  27.3 0.0 collective-permute-done.rest_0_
  27.3 0.0 all-to-all-done.down
  27.3 0.0 copy-done.1
  27.3 0.0 copy-done.2
  27.3 0.0 copy-done.3
  27.3 0.3 dispatch.1
  27.6 12.9 %all_to_all.32 = bf16[8,24,256]{2,1,0:T(8,128)(2,1)S(1)} all-to-all(bf16[8,24,256]{2,1,0:T(8,128)(2,1)S(1)} %bitcast.15), channel_id=1, replica_groups=mesh['req'=8,'head'=4] {'req'}, dimensions={0} | all-to-all | bytes 196608 | tf_op jit(solution)/shard_map/all_to_all | solution.py:601
  40.5 0.0 copy-done
  40.5 1.2 %shared_in.1 = bf16[8,184,128]{2,1,0:T(8,128)(2,1)} custom-call(bf16[192,256]{1,0:T(8,128)(2,1)S(1)} %bitcast.13, bf16[2,256,1408]{2,1,0:T(8,128)(2,1)S(1)} %copy-done, bf16[64,128]{1,0:T(8,128)(2,1)S(1)} %get-tuple-element.22.meta), custom_call_target="tpu_custom_call" | custom-call | tf_op jit(solution)/shard_map/shared_in/pallas_call | solution.py:410
  41.7 3.4 %all-to-all-start.2 = ((bf16[8,184,128]{2,1,0:T(8,128)(2,1)}), bf16[8,184,128]{2,1,0:T(8,128)(2,1)S(1)}, u32[]{:S(2)}, u32[]{:S(2)}) async-start(bf16[8,184,128]{2,1,0:T(8,128)(2,1)} %shared_in.1), calls=%async_computation.2 | async-start | bytes 753664 | tf_op jit(solution)/shard_map/all_to_all | solution.py:603
  45.2 8.2 %experts.1.routed = f32[16,2048]{1,0:T(8,128)S(1)} custom-call(bf16[192,256]{1,0:T(8,128)(2,1)S(1)} %bitcast.14, bf16[2,1408,2048]{2,1,0:T(8,128)(2,1)} %gu_hbm.1, bf16[1408,2048]{1,0:T(8,128)(2,1)} %down_hbm.1), custom_call_target="tpu_custom_call" | custom-call | flops 276824064 | bytes 17301504 | tf_op jit(solution)/shard_map/experts/pallas_call | solution.py:467
  53.4 2.2 %all-to-all-done.2.sums = bf16[8,184,128]{2,1,0:T(8,128)(2,1)S(1)} async-done(((bf16[8,184,128]{2,1,0:T(8,128)(2,1)}), bf16[8,184,128]{2,1,0:T(8,128)(2,1)S(1)}, u32[]{:S(2)}, u32[]{:S(2)}) %all-to-all-start.2) | async-done | bytes 376864 | tf_op jit(solution)/shard_map/all_to_all | solution.py:603
  55.6 0.4 give_back.1
  56.0 13.5 %all_to_all.33 = bf16[32,8,512]{2,1,0:T(8,128)(2,1)S(1)} all-to-all(bf16[32,8,512]{2,1,0:T(8,128)(2,1)S(1)} %bitcast.12), channel_id=1, replica_groups=mesh['req'=8,'head'=4] {'req','head'}, dimensions={0} | all-to-all | bytes 524288 | tf_op jit(solution)/shard_map/all_to_all | solution.py:606
  69.5 0.6 finish.1
  (1 shorter events, 0.0 us)
Async XLA Ops:
  0.6 26.7 %all-to-all-start = ((bf16[8,176,256]{2,1,0:T(8,128)(2,1)}), bf16[8,176,256]{2,1,0:T(8,128)(2,1)S(1)}, u32[]{:S(2)}, u32[]{:S(2)}) async-start(bf16[8,176,256]{2,1,0:T(8,128)(2,1)} %bitcast.19), calls=%async_computation | async-start | bytes 1441792 | tf_op jit(solution)/shard_map/all_to_all | solution.py:576
  7.9 19.4 %copy-start.1 = (bf16[8,2048]{1,0:T(8,128)(2,1)S(1)}, bf16[8,2048]{1,0:T(8,128)(2,1)}, u32[]{:S(2)}) copy-start(bf16[8,2048]{1,0:T(8,128)(2,1)} %hidden.1) | copy-start | bytes 98308
  7.9 19.4 %copy-start.2 = (f32[2048]{0:T(1024)S(1)}, f32[2048]{0:T(1024)}, u32[]{:S(2)}) copy-start(f32[2048]{0:T(1024)} %param.26) | copy-start | bytes 24580
  7.9 19.4 %copy-start.3 = (f32[2048]{0:T(1024)S(1)}, f32[2048]{0:T(1024)}, u32[]{:S(2)}) copy-start(f32[2048]{0:T(1024)} %param.31) | copy-start | bytes 24580
  7.9 32.6 %copy-start = (bf16[2,256,1408]{2,1,0:T(8,128)(2,1)S(1)}, bf16[2,256,1408]{2,1,0:T(8,128)(2,1)}, u32[]{:S(2)}) copy-start(bf16[2,256,1408]{2,1,0:T(8,128)(2,1)} %weights.1) | copy-start | bytes 4325380
  22.3 5.0 %collective-permute-start = (f32[8,2048]{1,0:T(8,128)S(1)}, f32[8,2048]{1,0:T(8,128)S(1)}, u32[]{:S(2)}, u32[]{:S(2)}) collective-permute-start(f32[8,2048]{1,0:T(8,128)S(1)} %get-tuple-element.14.mine), channel_id=1, source_target_pairs={{0,1},{1,0},{2,3},{3,2},{4,5},{5,4},{6,7},{7,6},{8,9},{9,8},{10,11... | collective-permute-start | bytes 196616 | tf_op jit(solution)/shard_map/ppermute | solution.py:594
  22.4 4.0 %collective-permute-start.1 = (bf16[8,2048]{1,0:T(8,128)(2,1)S(1)}, bf16[8,2048]{1,0:T(8,128)(2,1)S(1)}, u32[]{:S(2)}, u32[]{:S(2)}) collective-permute-start(bf16[8,2048]{1,0:T(8,128)(2,1)S(1)} %get-tuple-element.17), channel_id=1, source_target_pairs={{0,2},{1,3},{2,0},{3,1},{4,6},{5,7},{6,4},{7,5},{8,10},{9,11},{10,... | collective-permute-start | bytes 98312 | tf_op jit(solution)/shard_map/ppermute | solution.py:594
  24.0 3.3 %collective-permute-start.2 = (bf16[8,2048]{1,0:T(8,128)(2,1)S(1)}, bf16[8,2048]{1,0:T(8,128)(2,1)S(1)}, u32[]{:S(2)}, u32[]{:S(2)}) collective-permute-start(bf16[8,2048]{1,0:T(8,128)(2,1)S(1)} %get-tuple-element.17), channel_id=1, source_target_pairs={{0,3},{1,2},{2,1},{3,0},{4,7},{5,6},{6,5},{7,4},{8,11},{9,10},{10,... | collective-permute-start | bytes 98312 | tf_op jit(solution)/shard_map/ppermute | solution.py:594
  41.7 13.9 %all-to-all-start.2 = ((bf16[8,184,128]{2,1,0:T(8,128)(2,1)}), bf16[8,184,128]{2,1,0:T(8,128)(2,1)S(1)}, u32[]{:S(2)}, u32[]{:S(2)}) async-start(bf16[8,184,128]{2,1,0:T(8,128)(2,1)} %shared_in.1), calls=%async_computation.2 | async-start | bytes 753664 | tf_op jit(solution)/shard_map/all_to_all | solution.py:603

commit v5 on v3

--- a/solution.py
+++ b/solution.py
@@ -603,7 +603,7 @@
     )
     parts = [
         lax.ppermute(part if k == 1 else low, "head", [(j, j ^ k) for j in range(heads_axis)])
-        for k in range(1, heads_axis)
+        for k in reversed(range(1, heads_axis))
     ]
     parts, down = lax.optimization_barrier((parts, down))
     send, own = dispatch(

time: 69.6 us -> 70.7 us (1.016)
  Pallas kernels: 24.2 us -> 25.2 us
  waiting for transfers between devices: 5.07 us -> 4.1 us
  blocking collectives: 26.5 us -> 27.3 us
    all_to_all x1, waiting for transfers between devices: 1.86 us -> 0.69 us  [local(): sums = lax.all_to_all(sums, 'req', split_axis=0, concat_axis=0, tiled=True)]
    pallas_call x1, Pallas kernels: 13.5 us -> 14.5 us  [attend(): pl.pallas_call(functools.partial(attend_kernel, groups, heads_axis), out_...]
    all_to_all x1, blocking collectives: 13.9 us -> 14.8 us  [local(): lax.all_to_all(back, ('req', 'head'), split_axis=0, concat_axis=0, tiled=...]
  transfers between devices with their start and end apart: 5 -> 5, of which waited for: 4 -> 3; matrix products, arithmetic and copies ran while one was open for 0% -> 0% of each run, Pallas kernels for 31% -> 32%
where the time goes in v5:
time: 70.7 us; the launch traced here: 70.3 us
  blocking collectives  27.3 us (39%)
  Pallas kernels  25.2 us (36%)
  starting transfers between devices  12.9 us (18%)
  waiting for transfers between devices  4.1 us (6%)
  between operations  0.74 us (1%)
    all_to_all x1, blocking collectives, local(): lax.all_to_all(back, ('req', 'head'), split_axis=0, concat_axis=0, tiled=...  14.8 us
    pallas_call x1, Pallas kernels, attend(): pl.pallas_call(functools.partial(attend_kernel, groups, heads_axis), out_...  14.5 us
    all_to_all x1, blocking collectives, local(): lax.all_to_all(send, 'req', split_axis=0, concat_axis=0, tiled=True)  12.5 us
    pallas_call x1, Pallas kernels, experts(): pl.pallas_call(functools.partial(expert_kernel, groups, rows), out_shape=...  8.23 us
    all_to_all x1, starting transfers between devices, local(): down = lax.all_to_all(down, 'req', split_axis=0, concat_axis=0, tiled=True)  7.26 us
    all_to_all x1, starting transfers between devices, local(): sums = lax.all_to_all(sums, 'req', split_axis=0, concat_axis=0, tiled=True)  3.45 us
    ppermute x3, waiting for transfers between devices, local(): lax.ppermute(part if k == 1 else low, 'head', [(j, j ^ k) for j in range(...  3.41 us
    ppermute x3, starting transfers between devices, local(): lax.ppermute(part if k == 1 else low, 'head', [(j, j ^ k) for j in range(...  2.21 us
  transfers between devices with their start and end apart: 5, of which 3 were waited for; matrix products, arithmetic and copies ran while one was open for 0% of the time, Pallas kernels for 32%

profile of v5, /device:TPU:0, one launch (start us, length us, event | category | flops | bytes accessed | tf_op | source)
XLA Modules:
  0.0 70.3 jit_solution(13066136705894418277)
XLA Ops:
  0.6 7.3 %all-to-all-start = ((bf16[8,176,256]{2,1,0:T(8,128)(2,1)}), bf16[8,176,256]{2,1,0:T(8,128)(2,1)S(1)}, u32[]{:S(2)}, u32[]{:S(2)}) async-start(bf16[8,176,256]{2,1,0:T(8,128)(2,1)} %bitcast.21), calls=%async_computation | async-start | bytes 1441792 | tf_op jit(solution)/shard_map/all_to_all | solution.py:587
  7.9 0.0 copy-start.1
  7.9 0.0 copy-start.2
  7.9 0.0 copy-start.3
  7.9 0.0 copy-start
  8.0 14.5 %attend.1 = (f32[8,2048]{1,0:T(8,128)S(1)}, bf16[8,2048]{1,0:T(8,128)(2,1)S(1)}, bf16[8,2,512]{2,1,0:T(2,128)(2,1)}, bf16[192,64]{1,0:T(8,128)(2,1)S(1)}, bf16[64,256]{1,0:T(8,128)(2,1)S(1)}) custom-call(f32[1,64]{1,0:T(1,128)S(1)} %multiply_power_fusion.freq, s32[8]{0:T(128)} %lens_hbm.1, bf16[8,2048]{1,0:T(8,128)(2,1)} %hidden.1, f32[1,2048]{1,0:T(1,128)} %bitcast.22, ...), custom_call_target="tpu_custom_call" | custom-call | tf_op jit(solution)/shard_map/attend/pallas_call | solution.py:317
  22.5 0.1 collective-permute-start.2
  22.6 1.6 %collective-permute-start = (bf16[8,2048]{1,0:T(8,128)(2,1)S(1)}, bf16[8,2048]{1,0:T(8,128)(2,1)S(1)}, u32[]{:S(2)}, u32[]{:S(2)}) collective-permute-start(bf16[8,2048]{1,0:T(8,128)(2,1)S(1)} %get-tuple-element.16), channel_id=1, source_target_pairs={{0,3},{1,2},{2,1},{3,0},{4,7},{5,6},{6,5},{7,4},{8,11},{9,10},{10,... | collective-permute-start | bytes 98312 | tf_op jit(solution)/shard_map/ppermute | solution.py:605
  24.2 0.5 collective-permute-start.1
  24.7 1.3 %collective-permute-done.rest_0_ = bf16[8,2048]{1,0:T(8,128)(2,1)S(1)} collective-permute-done((bf16[8,2048]{1,0:T(8,128)(2,1)S(1)}, bf16[8,2048]{1,0:T(8,128)(2,1)S(1)}, u32[]{:S(2)}, u32[]{:S(2)}) %collective-permute-start) | collective-permute-done | bytes 32800 | tf_op jit(solution)/shard_map/ppermute | solution.py:605
  26.0 2.1 %collective-permute-done.1.rest_1_ = bf16[8,2048]{1,0:T(8,128)(2,1)S(1)} collective-permute-done((bf16[8,2048]{1,0:T(8,128)(2,1)S(1)}, bf16[8,2048]{1,0:T(8,128)(2,1)S(1)}, u32[]{:S(2)}, u32[]{:S(2)}) %collective-permute-start.1) | collective-permute-done | bytes 32800 | tf_op jit(solution)/shard_map/ppermute | solution.py:605
  28.1 0.0 collective-permute-done.2.rest_2_
  28.1 0.0 all-to-all-done.down
  28.1 0.0 copy-done.1
  28.1 0.0 copy-done.2
  28.2 0.0 copy-done.3
  28.2 0.3 dispatch.1
  28.4 12.5 %all_to_all.32 = bf16[8,32,256]{2,1,0:T(8,128)(2,1)S(1)} all-to-all(bf16[8,32,256]{2,1,0:T(8,128)(2,1)S(1)} %bitcast.17), channel_id=1, replica_groups=mesh['req'=8,'head'=4] {'req'}, dimensions={0} | all-to-all | bytes 262144 | tf_op jit(solution)/shard_map/all_to_all | solution.py:612
  41.0 0.0 copy-done
  41.0 1.1 %shared_in.1 = bf16[1408,128]{1,0:T(8,128)(2,1)} custom-call(bf16[256,256]{1,0:T(8,128)(2,1)S(1)} %bitcast.12, bf16[2,256,1408]{2,1,0:T(8,128)(2,1)S(1)} %copy-done), custom_call_target="tpu_custom_call" | custom-call | tf_op jit(solution)/shard_map/shared_in/pallas_call | solution.py:417
  42.1 3.5 %all-to-all-start.2 = ((bf16[8,176,128]{2,1,0:T(8,128)(2,1)}), bf16[8,176,128]{2,1,0:T(8,128)(2,1)S(1)}, u32[]{:S(2)}, u32[]{:S(2)}) async-start(bf16[8,176,128]{2,1,0:T(8,128)(2,1)} %bitcast.9), calls=%async_computation.2 | async-start | bytes 720896 | tf_op jit(solution)/shard_map/all_to_all | solution.py:615
  45.6 8.2 %experts.1.routed = f32[16,2048]{1,0:T(8,128)S(1)} custom-call(bf16[256,256]{1,0:T(8,128)(2,1)S(1)} %bitcast.13, bf16[2,1408,2048]{2,1,0:T(8,128)(2,1)} %gu_hbm.1, bf16[1408,2048]{1,0:T(8,128)(2,1)} %down_hbm.1), custom_call_target="tpu_custom_call" | custom-call | flops 276824064 | bytes 17301504 | tf_op jit(solution)/shard_map/experts/pallas_call | solution.py:478
  53.8 0.7 all-to-all-done.2.sums
  54.5 0.4 give_back.1
  54.9 14.8 %all_to_all.33 = bf16[32,8,512]{2,1,0:T(8,128)(2,1)S(1)} all-to-all(bf16[32,8,512]{2,1,0:T(8,128)(2,1)S(1)} %bitcast.15), channel_id=1, replica_groups=mesh['req'=8,'head'=4] {'req','head'}, dimensions={0} | all-to-all | bytes 524288 | tf_op jit(solution)/shard_map/all_to_all | solution.py:618
  69.7 0.6 finish.1
  (1 shorter events, 0.0 us)
Async XLA Ops:
  0.6 27.5 %all-to-all-start = ((bf16[8,176,256]{2,1,0:T(8,128)(2,1)}), bf16[8,176,256]{2,1,0:T(8,128)(2,1)S(1)}, u32[]{:S(2)}, u32[]{:S(2)}) async-start(bf16[8,176,256]{2,1,0:T(8,128)(2,1)} %bitcast.21), calls=%async_computation | async-start | bytes 1441792 | tf_op jit(solution)/shard_map/all_to_all | solution.py:587
  7.9 20.2 %copy-start.1 = (bf16[8,2048]{1,0:T(8,128)(2,1)S(1)}, bf16[8,2048]{1,0:T(8,128)(2,1)}, u32[]{:S(2)}) copy-start(bf16[8,2048]{1,0:T(8,128)(2,1)} %hidden.1) | copy-start | bytes 98308
  7.9 20.2 %copy-start.2 = (f32[2048]{0:T(1024)S(1)}, f32[2048]{0:T(1024)}, u32[]{:S(2)}) copy-start(f32[2048]{0:T(1024)} %param.26) | copy-start | bytes 24580
  7.9 20.2 %copy-start.3 = (f32[2048]{0:T(1024)S(1)}, f32[2048]{0:T(1024)}, u32[]{:S(2)}) copy-start(f32[2048]{0:T(1024)} %param.31) | copy-start | bytes 24580
  7.9 33.0 %copy-start = (bf16[2,256,1408]{2,1,0:T(8,128)(2,1)S(1)}, bf16[2,256,1408]{2,1,0:T(8,128)(2,1)}, u32[]{:S(2)}) copy-start(bf16[2,256,1408]{2,1,0:T(8,128)(2,1)} %weights.1) | copy-start | bytes 4325380
  22.5 5.6 %collective-permute-start.2 = (f32[8,2048]{1,0:T(8,128)S(1)}, f32[8,2048]{1,0:T(8,128)S(1)}, u32[]{:S(2)}, u32[]{:S(2)}) collective-permute-start(f32[8,2048]{1,0:T(8,128)S(1)} %get-tuple-element.13.mine), channel_id=1, source_target_pairs={{0,1},{1,0},{2,3},{3,2},{4,5},{5,4},{6,7},{7,6},{8,9},{9,8},{10,11... | collective-permute-start | bytes 196616 | tf_op jit(solution)/shard_map/ppermute | solution.py:605
  22.6 3.4 %collective-permute-start = (bf16[8,2048]{1,0:T(8,128)(2,1)S(1)}, bf16[8,2048]{1,0:T(8,128)(2,1)S(1)}, u32[]{:S(2)}, u32[]{:S(2)}) collective-permute-start(bf16[8,2048]{1,0:T(8,128)(2,1)S(1)} %get-tuple-element.16), channel_id=1, source_target_pairs={{0,3},{1,2},{2,1},{3,0},{4,7},{5,6},{6,5},{7,4},{8,11},{9,10},{10,... | collective-permute-start | bytes 98312 | tf_op jit(solution)/shard_map/ppermute | solution.py:605
  24.2 3.9 %collective-permute-start.1 = (bf16[8,2048]{1,0:T(8,128)(2,1)S(1)}, bf16[8,2048]{1,0:T(8,128)(2,1)S(1)}, u32[]{:S(2)}, u32[]{:S(2)}) collective-permute-start(bf16[8,2048]{1,0:T(8,128)(2,1)S(1)} %get-tuple-element.16), channel_id=1, source_target_pairs={{0,2},{1,3},{2,0},{3,1},{4,6},{5,7},{6,4},{7,5},{8,10},{9,11},{10,... | collective-permute-start | bytes 98312 | tf_op jit(solution)/shard_map/ppermute | solution.py:605
  42.1 12.4 %all-to-all-start.2 = ((bf16[8,176,128]{2,1,0:T(8,128)(2,1)}), bf16[8,176,128]{2,1,0:T(8,128)(2,1)S(1)}, u32[]{:S(2)}, u32[]{:S(2)}) async-start(bf16[8,176,128]{2,1,0:T(8,128)(2,1)} %bitcast.9), calls=%async_computation.2 | async-start | bytes 720896 | tf_op jit(solution)/shard_map/all_to_all | solution.py:615
